TPU v7x, 128 devices: a whole 4x4x4 slice. The times are simulated.
128 devices in a mesh: seq: 8 (over y, core), exp: 16 (over z, x).
Axes of the slice: x: 4, y: 4, z: 4, core: 2. Of those that a mesh axis runs over, the one named last changes fastest.
Arguments:
- queries: bfloat16 [4096, 4096], P('seq', 'exp'), may hold values from -6 to 6
- key_rows: bfloat16 [4096, 512], P('seq', 'exp'), may hold values from -6 to 6
- value_rows: bfloat16 [4096, 512], P('seq', 'exp'), may hold values from -6 to 6
- sink_logits: float32 [64], P('exp'), may hold values from 0 to 6
- out_proj: bfloat16 [4096, 2560], P('exp'), may hold values from -0.09375 to 0.09375
- residual: bfloat16 [4096, 2560], P(('seq', 'exp')), may hold values from -0.59765625 to 0.59765625
- norm_gain: float32 [2560], replicated, may hold values from 0.25 to 1.75
- expert_ids: int32 [4096, 4], P(('seq', 'exp')), may hold values from 0 to 127, all different within a row; in each aligned block of 32 rows (0 to 31, 32 to 63, ...) at most 2 rows name the same one
- gate_weights: float32 [4096, 4], P(('seq', 'exp')), may hold values from 0.2 to 1
- w_gate_up: bfloat16 [128, 2560, 2880], P(('seq', 'exp')), may hold values from -0.125 to 0.125
- w_down: bfloat16 [128, 1440, 2560], P(('seq', 'exp')), may hold values from -0.15625 to 0.15625
Outputs:
- layer_out: bfloat16 [4096, 2560], P(('seq', 'exp'))
Inputs may be any that keep to these rules, and one draw needn't show every extreme that they name: `expert_ids`: each row names 4 different experts. In the rows of one device (aligned blocks of 32 rows) no expert is named more than 2 times, and in every draw some expert is named exactly 2 times in some block.
All inputs are finite; a program needn't handle non-finite values.
Results may differ from a plain program's by a relative error of at most 0.022.
Values may be sent and summed in bfloat16 or wider, within the bound.
A program may use at most 128 MiB of HBM per device.

v0:
```python
import math

import jax
import jax.numpy as jnp
from jax import lax
from jax.sharding import PartitionSpec as P

D = 2560
WINDOW = 128


def swapped(value, axis, apart):
    return lax.ppermute(value, axis, [(i, i ^ 1 << apart) for i in range(lax.axis_size(axis))])


def shifted(block, axis, distance):
    devices = range(lax.axis_size(axis))
    route = [(i - distance, i) for i in devices if i - distance in devices]
    return lax.ppermute(block, axis, route)


def split_up(value, dim, length):
    lengths = value.shape
    parts = value.reshape(*lengths[:dim], length, lengths[dim] // length, *lengths[dim + 1 :])
    return jnp.moveaxis(parts, dim, 0)


def sent_and_summed(value, axis, dim):
    length = lax.axis_size(axis)
    parts = lax.all_to_all(split_up(value, dim, length), axis, 0, 0, tiled=True)
    return jnp.sum(parts.astype(jnp.float32), axis=0)


def window_attention(
    query_rows, key_block, value_block, prior_keys, prior_values, sink_row, first_index, window_size
):
    row_count = query_rows.shape[0]
    head_width_dim = key_block.shape[1]
    head_count = query_rows.shape[1] // head_width_dim
    block_count = row_count // window_size
    key_ext = jnp.concatenate([prior_keys, key_block], axis=0)
    value_ext = jnp.concatenate([prior_values, value_block], axis=0)
    key_block_tiles = jnp.concatenate(
        [
            key_ext[:row_count].reshape(block_count, window_size, head_width_dim),
            key_block.reshape(block_count, window_size, head_width_dim),
        ],
        axis=1,
    )
    value_block_tiles = jnp.concatenate(
        [
            value_ext[:row_count].reshape(block_count, window_size, head_width_dim),
            value_block.reshape(block_count, window_size, head_width_dim),
        ],
        axis=1,
    )
    query_block_tiles = query_rows.reshape(block_count, window_size, head_count, head_width_dim)
    attention_scores = jnp.einsum(
        "xnem,xcm->xenc", query_block_tiles, key_block_tiles, preferred_element_type=jnp.float32
    ) * (1.0 / math.sqrt(head_width_dim))
    query_pos = jnp.arange(window_size, dtype=jnp.int32)[:, None]
    key_pos = jnp.arange(2 * window_size, dtype=jnp.int32)[None, :]
    inside = (key_pos > query_pos) & (key_pos <= query_pos + window_size)
    block_start = first_index + jnp.arange(block_count, dtype=jnp.int32) * window_size
    present = block_start[:, None] - window_size + key_pos >= 0
    allowed = inside[None, None, :, :] & present[:, None, None, :]
    attention_scores = jnp.where(allowed, attention_scores, -jnp.inf)
    sink_grid = sink_row[None, :, None, None]
    highest = jnp.maximum(jnp.max(attention_scores, axis=-1, keepdims=True), sink_grid)
    raised = jnp.exp(attention_scores - highest)
    totals = jnp.sum(raised, axis=-1, keepdims=True) + jnp.exp(sink_grid - highest)
    attention_probabilities = (raised / totals).astype(jnp.bfloat16)
    mixed_value_rows = jnp.einsum(
        "emjt,eta->ejma",
        attention_probabilities,
        value_block_tiles,
        preferred_element_type=jnp.float32,
    )
    return mixed_value_rows.astype(jnp.bfloat16).reshape(row_count, head_count * head_width_dim)


def expert_rows(rows_in, gate_up, down_rows):
    hidden_units = gate_up.shape[1] // 2
    both = jnp.dot(rows_in, gate_up, preferred_element_type=jnp.float32)
    gate_part = both[:, :hidden_units]
    up_part = both[:, hidden_units:]
    activated = (gate_part * jax.nn.sigmoid(1.702 * gate_part) * (up_part + 1.0)).astype(
        jnp.bfloat16
    )
    return jnp.dot(activated, down_rows, preferred_element_type=jnp.float32).astype(jnp.bfloat16)


def per_device(
    queries,
    key_rows,
    value_rows,
    sink_logits,
    out_proj,
    residual,
    norm_gain,
    expert_ids,
    gate_weights,
    w_gate_up,
    w_down,
):
    seq_index = lax.axis_index("seq")
    exp_index = lax.axis_index("exp")
    local_rows = queries.shape[0]
    key_piece = key_rows
    value_piece = value_rows
    other_keys, other_values = swapped((key_piece, value_piece), "exp", 0)
    upper_half = jnp.right_shift(exp_index, 0) & 1 == 1
    key_piece = jnp.where(
        upper_half,
        jnp.concatenate([other_keys, key_piece], axis=1),
        jnp.concatenate([key_piece, other_keys], axis=1),
    )
    value_piece = jnp.where(
        upper_half,
        jnp.concatenate([other_values, value_piece], axis=1),
        jnp.concatenate([value_piece, other_values], axis=1),
    )
    prior_keys, prior_values = shifted(
        (key_piece[local_rows - WINDOW :], value_piece[local_rows - WINDOW :]), "seq", 1
    )
    attended = window_attention(
        queries,
        key_piece,
        value_piece,
        prior_keys,
        prior_values,
        sink_logits,
        seq_index * local_rows,
        WINDOW,
    )
    token_rows = local_rows // lax.axis_size("exp")
    projected = sent_and_summed(
        jnp.dot(attended, out_proj, preferred_element_type=jnp.float32).astype(jnp.bfloat16),
        "exp",
        0,
    )
    hidden = residual.astype(jnp.float32) + projected
    scale = lax.rsqrt(jnp.mean(hidden * hidden, axis=-1, keepdims=True) + 1e-05)
    normed = (hidden * scale * norm_gain[None, :]).astype(jnp.bfloat16)
    expert_total = lax.axis_size("seq") * lax.axis_size("exp")
    top_count = expert_ids.shape[1]
    slot_count = 2 * top_count * token_rows // expert_total
    flat_ids = expert_ids.reshape(-1)
    chosen = (flat_ids[:, None] == jnp.arange(expert_total, dtype=jnp.int32)[None, :]).astype(
        jnp.int32
    )
    slot_rank = jnp.sum((jnp.cumsum(chosen, axis=0) - chosen) * chosen, axis=1)
    slot_index = flat_ids * slot_count + slot_rank
    placing = jnp.arange(expert_total * slot_count, dtype=jnp.int32)[:, None] == slot_index[None, :]
    dispatch = jnp.any(
        placing.reshape(expert_total * slot_count, token_rows, top_count), axis=2
    ).astype(jnp.bfloat16)
    outgoing = (
        jnp.dot(dispatch, normed, preferred_element_type=jnp.float32)
        .astype(jnp.bfloat16)
        .reshape(expert_total, slot_count, D)
    )
    gate_up = w_gate_up[0]
    down_rows = w_down[0]
    arrived = lax.all_to_all(outgoing, ("seq", "exp"), split_axis=0, concat_axis=0, tiled=True)
    sources = arrived.shape[0]
    slots_here = arrived.shape[1]
    result = expert_rows(arrived.reshape(sources * slots_here, D), gate_up, down_rows).reshape(
        sources, slots_here, D
    )
    returned = lax.all_to_all(result, ("seq", "exp"), split_axis=0, concat_axis=0, tiled=True)
    picked = returned.reshape(expert_total * slot_count, D)[slot_index]
    weighted = jnp.sum(
        gate_weights[:, :, None] * picked.reshape(token_rows, top_count, D).astype(jnp.float32),
        axis=1,
    )
    return (hidden + weighted).astype(jnp.bfloat16)


def solution(mesh):
    return jax.shard_map(
        per_device,
        mesh=mesh,
        in_specs=(
            P("seq", "exp"),
            P("seq", "exp"),
            P("seq", "exp"),
            P("exp"),
            P("exp", None),
            P(("seq", "exp"), None),
            P(),
            P(("seq", "exp"), None),
            P(("seq", "exp"), None),
            P(("seq", "exp"), None, None),
            P(("seq", "exp"), None, None),
        ),
        out_specs=P(("seq", "exp"), None),
        check_vma=False,
    )
```

profile of v0, /device:TPU:1, one launch (start us, length us, event | category | flops | bytes accessed | tf_op | source)
XLA Modules:
  0.0 147.8 jit_solution(16556722022525732065)
XLA Ops:
  0.0 2.0 %collective-permute-start.2 = (bf16[512,32]{0,1:T(8,128)(2,1)}, bf16[512,32]{0,1:T(8,128)(2,1)S(1)}, u32[]{:S(2)}, u32[]{:S(2)}) collective-permute-start(bf16[512,32]{0,1:T(8,128)(2,1)} %param.12), channel_id=1, source_target_pairs={{0,1},{1,0},{2,3},{3,2},{4,5},{5,4},{6,7},{7,6},{8,9},{9,8},{10,11... | collective-permute-start | bytes 98312 | tf_op jit(solution)/shard_map/ppermute | solution.py:13
  2.1 0.8 copy_bitcast_fusion.2
  3.0 0.2 broadcast_and_fusion
  3.2 0.8 copy_bitcast_fusion.4
  4.0 1.2 reshape.202
  5.3 0.9 maximum_select_fusion.2
  6.1 4.5 %collective-permute-start.3 = (bf16[128,64]{0,1:T(8,128)(2,1)S(1)}, bf16[128,64]{0,1:T(8,128)(2,1)S(1)}, u32[]{:S(2)}, u32[]{:S(2)}) collective-permute-start(bf16[128,64]{0,1:T(8,128)(2,1)S(1)} %slice.27), channel_id=1, source_target_pairs={{0,16},{16,32},{32,48},{48,64},{64,80},{80,96},{96,112},{1,17},{17... | collective-permute-start | bytes 49160 | tf_op jit(solution)/shard_map/ppermute | solution.py:19
  10.7 0.9 maximum_select_fusion
  11.5 1.9 %collective-permute-start.1 = (bf16[128,64]{0,1:T(8,128)(2,1)S(1)}, bf16[128,64]{0,1:T(8,128)(2,1)S(1)}, u32[]{:S(2)}, u32[]{:S(2)}) collective-permute-start(bf16[128,64]{0,1:T(8,128)(2,1)S(1)} %slice.26), channel_id=1, source_target_pairs={{0,16},{16,32},{32,48},{48,64},{64,80},{80,96},{96,112},{1,17},{17... | collective-permute-start | bytes 49160 | tf_op jit(solution)/shard_map/ppermute | solution.py:19
  13.6 0.5 fusion.34
  14.2 0.3 fusion.7
  14.6 0.5 fusion.10
  15.1 0.2 copy.47
  15.3 2.4 %convolution_convert_fusion = bf16[512,2560]{1,0:T(8,128)(2,1)} fusion(bf16[256,2560]{1,0:T(8,128)(2,1)S(1)} %copy-done, bf16[32,8,4,128]{3,2,1,0:T(4,128)(2,1)S(1)} %bitcast.72), kind=kOutput, calls=%fused_computation.6 | convolution fusion | flops 672399360 | bytes 4194304 | tf_op jit(solution)/shard_map/dot_general | solution.py:138
  17.7 7.8 %all-to-all-start = ((bf16[16,32,2560]{2,1,0:T(8,128)(2,1)}), bf16[16,32,2560]{2,1,0:T(8,128)(2,1)}, u32[]{:S(2)}, u32[]{:S(2)}) async-start(bf16[16,32,2560]{2,1,0:T(8,128)(2,1)} %bitcast.71), calls=%async_computation | async-start | bytes 5242880 | tf_op jit(solution)/shard_map/all_to_all | solution.py:30
  25.8 0.2 reduce_window_sum.11
  26.5 38.6 %all-to-all-done = bf16[16,32,2560]{2,1,0:T(8,128)(2,1)} async-done(((bf16[16,32,2560]{2,1,0:T(8,128)(2,1)}), bf16[16,32,2560]{2,1,0:T(8,128)(2,1)}, u32[]{:S(2)}, u32[]{:S(2)}) %all-to-all-start) | async-done | bytes 2621472 | tf_op jit(solution)/shard_map/all_to_all | solution.py:30
  65.1 2.1 %convert_reduce_fusion = f32[32,2560]{1,0:T(8,128)S(1)} fusion(bf16[16,32,2560]{2,1,0:T(8,128)(2,1)} %all-to-all-done), kind=kLoop, calls=%fused_computation.5 | loop fusion | flops 2539520 | bytes 2949120 | tf_op jit(solution)/shard_map/reduce_sum | solution.py:31
  67.4 0.6 convolution_convert_fusion.1
  68.0 1.4 reshape.187
  69.4 26.9 %all_to_all.15 = bf16[128,2,2560]{2,1,0:T(2,128)(2,1)S(1)} all-to-all(bf16[128,2,2560]{2,1,0:T(2,128)(2,1)} %reshape.187), channel_id=1, replica_groups=mesh['seq'=8,'exp'=16] {'seq','exp'}, dimensions={0} | all-to-all | bytes 2621440 | tf_op jit(solution)/shard_map/all_to_all | solution.py:165
  96.3 1.4 reshape.188
  97.6 8.0 %fusion = f32[256,2880]{0,1:T(8,128)S(1)} fusion(bf16[256,2560]{1,0:T(8,128)(2,1)} %reshape.188, bf16[1,2560,2880]{1,2,0:T(8,128)(2,1)} %param.20), kind=kOutput, calls=%fused_computation.1 | convolution fusion | flops 3774873600 | bytes 19005440 | tf_op jit(solution)/shard_map/dot_general | solution.py:84
  105.6 5.5 %fusion.4 = bf16[256,2560]{1,0:T(8,128)(2,1)S(1)} fusion(bf16[1,1440,2560]{2,1,0:T(8,128)(2,1)} %param.21, f32[256,2880]{0,1:T(8,128)S(1)} %fusion), kind=kOutput, calls=%fused_computation.8 | convolution fusion | flops 1891041280 | bytes 11632640 | tf_op jit(solution)/shard_map/dot_general | solution.py:90
  111.1 1.4 reshape.189
  112.4 5.8 %all-to-all-start.2 = ((bf16[128,2,2560]{2,1,0:T(2,128)(2,1)}), bf16[128,2,2560]{2,1,0:T(2,128)(2,1)}, u32[]{:S(2)}, u32[]{:S(2)}) async-start(bf16[128,2,2560]{2,1,0:T(2,128)(2,1)} %reshape.189), calls=%async_computation.2 | async-start | bytes 2621440 | tf_op jit(solution)/shard_map/all_to_all | solution.py:171
  118.4 21.1 %all-to-all-done.2 = bf16[128,2,2560]{2,1,0:T(2,128)(2,1)} async-done(((bf16[128,2,2560]{2,1,0:T(2,128)(2,1)}), bf16[128,2,2560]{2,1,0:T(2,128)(2,1)}, u32[]{:S(2)}, u32[]{:S(2)}) %all-to-all-start.2) | async-done | bytes 1310752 | tf_op jit(solution)/shard_map/all_to_all | solution.py:171
  139.6 3.2 %reshape.190 = bf16[256,2560]{1,0:T(8,128)(2,1)S(1)} reshape(bf16[128,2,2560]{2,1,0:T(2,128)(2,1)} %all-to-all-done.2) | data formatting | bytes 2621440 | tf_op jit(solution)/shard_map/reshape | solution.py:172
  142.7 1.8 %gather_fusion = bf16[128,2560]{1,0:T(8,128)(2,1)} fusion(bf16[256,2560]{1,0:T(8,128)(2,1)S(1)} %reshape.190, s32[1024]{0:T(1024)S(1)} %pad_clamp_fusion), kind=kCustom, calls=%fused_computation | custom fusion | bytes 1311232 | tf_op jit(solution)/shard_map/gather | solution.py:172
  144.6 1.6 %reshape.191 = f32[32,4,2560]{2,1,0:T(4,128)S(1)} reshape(bf16[128,2560]{1,0:T(8,128)(2,1)} %gather_fusion) | data formatting | bytes 1966080 | tf_op jit(solution)/shard_map/convert_element_type | solution.py:174
  146.1 0.9 multiply_reduce_fusion
  147.0 0.7 add_convert_fusion
  (44 shorter events, 1.6 us)
Async XLA Ops:
  0.0 15.3 %copy-start = (bf16[256,2560]{1,0:T(8,128)(2,1)S(1)}, bf16[256,2560]{1,0:T(8,128)(2,1)}, u32[]{:S(2)}) copy-start(bf16[256,2560]{1,0:T(8,128)(2,1)} %param.15) | copy-start | bytes 3932164
  0.0 5.3 %collective-permute-start.2 = (bf16[512,32]{0,1:T(8,128)(2,1)}, bf16[512,32]{0,1:T(8,128)(2,1)S(1)}, u32[]{:S(2)}, u32[]{:S(2)}) collective-permute-start(bf16[512,32]{0,1:T(8,128)(2,1)} %param.12), channel_id=1, source_target_pairs={{0,1},{1,0},{2,3},{3,2},{4,5},{5,4},{6,7},{7,6},{8,9},{9,8},{10,11... | collective-permute-start | bytes 98312 | tf_op jit(solution)/shard_map/ppermute | solution.py:13
  2.0 8.6 %collective-permute-start = (bf16[512,32]{0,1:T(8,128)(2,1)}, bf16[512,32]{0,1:T(8,128)(2,1)S(1)}, u32[]{:S(2)}, u32[]{:S(2)}) collective-permute-start(bf16[512,32]{0,1:T(8,128)(2,1)} %param.13), channel_id=1, source_target_pairs={{0,1},{1,0},{2,3},{3,2},{4,5},{5,4},{6,7},{7,6},{8,9},{9,8},{10,11... | collective-permute-start | bytes 98312 | tf_op jit(solution)/shard_map/ppermute | solution.py:13
  5.2 8.8 %copy-start.5 = (f32[4]{0:T(128)S(1)}, f32[4]{0:T(128)}, u32[]{:S(2)}) copy-start(f32[4]{0:T(128)} %param.14) | copy-start | bytes 52
  6.1 7.4 %collective-permute-start.3 = (bf16[128,64]{0,1:T(8,128)(2,1)S(1)}, bf16[128,64]{0,1:T(8,128)(2,1)S(1)}, u32[]{:S(2)}, u32[]{:S(2)}) collective-permute-start(bf16[128,64]{0,1:T(8,128)(2,1)S(1)} %slice.27), channel_id=1, source_target_pairs={{0,16},{16,32},{32,48},{48,64},{64,80},{80,96},{96,112},{1,17},{17... | collective-permute-start | bytes 49160 | tf_op jit(solution)/shard_map/ppermute | solution.py:19
  11.5 3.1 %collective-permute-start.1 = (bf16[128,64]{0,1:T(8,128)(2,1)S(1)}, bf16[128,64]{0,1:T(8,128)(2,1)S(1)}, u32[]{:S(2)}, u32[]{:S(2)}) collective-permute-start(bf16[128,64]{0,1:T(8,128)(2,1)S(1)} %slice.26), channel_id=1, source_target_pairs={{0,16},{16,32},{32,48},{48,64},{64,80},{80,96},{96,112},{1,17},{17... | collective-permute-start | bytes 49160 | tf_op jit(solution)/shard_map/ppermute | solution.py:19
  17.7 7.8 %copy-start.3 = (s32[32,4]{0,1:T(4,128)S(1)}, s32[32,4]{0,1:T(4,128)}, u32[]{:S(2)}) copy-start(s32[32,4]{0,1:T(4,128)} %param.18) | copy-start | bytes 1540
  17.7 47.3 %all-to-all-start = ((bf16[16,32,2560]{2,1,0:T(8,128)(2,1)}), bf16[16,32,2560]{2,1,0:T(8,128)(2,1)}, u32[]{:S(2)}, u32[]{:S(2)}) async-start(bf16[16,32,2560]{2,1,0:T(8,128)(2,1)} %bitcast.71), calls=%async_computation | async-start | bytes 5242880 | tf_op jit(solution)/shard_map/all_to_all | solution.py:30
  25.5 41.7 %copy-start.1 = (bf16[32,2560]{1,0:T(8,128)(2,1)S(1)}, bf16[32,2560]{1,0:T(8,128)(2,1)}, u32[]{:S(2)}) copy-start(bf16[32,2560]{1,0:T(8,128)(2,1)} %param.16) | copy-start | bytes 491524
  25.5 41.9 %copy-start.2 = (f32[2560]{0:T(1024)S(1)}, f32[2560]{0:T(1024)}, u32[]{:S(2)}) copy-start(f32[2560]{0:T(1024)} %param.17) | copy-start | bytes 30724
  111.1 7.3 %copy-start.4 = (f32[32,4]{0,1:T(4,128)S(1)}, f32[32,4]{0,1:T(4,128)}, u32[]{:S(2)}) copy-start(f32[32,4]{0,1:T(4,128)} %param.19) | copy-start | bytes 1540
  112.4 27.1 %all-to-all-start.2 = ((bf16[128,2,2560]{2,1,0:T(2,128)(2,1)}), bf16[128,2,2560]{2,1,0:T(2,128)(2,1)}, u32[]{:S(2)}, u32[]{:S(2)}) async-start(bf16[128,2,2560]{2,1,0:T(2,128)(2,1)} %reshape.189), calls=%async_computation.2 | async-start | bytes 2621440 | tf_op jit(solution)/shard_map/all_to_all | solution.py:171
where the time goes:
time: 149 us; the launch traced here: 148 us
  waiting for transfers between devices  59.8 us (40%)
  blocking collectives  26.9 us (18%)
  starting transfers between devices  22.1 us (15%)
  matrix products  17.4 us (12%)
  local copies, waits for them, and re-layouts  14.3 us (10%)
  other arithmetic  7 us (5%)
    all_to_all x1, waiting for transfers between devices, sent_and_summed(): parts = lax.all_to_all(split_up(value, dim, length), axis, 0, 0, tiled=True)  38.6 us
    all_to_all x1, blocking collectives, per_device(): lax.all_to_all(outgoing, ('seq', 'exp'), split_axis=0, concat_axis=0, til...  26.9 us
    all_to_all x1, waiting for transfers between devices, per_device(): lax.all_to_all(result, ('seq', 'exp'), split_axis=0, concat_axis=0, tiled...  21.1 us
    dot_general x1, matrix products, expert_rows(): both = jnp.dot(rows_in, gate_up, preferred_element_type=jnp.float32)  7.98 us
    all_to_all x1, starting transfers between devices, sent_and_summed(): parts = lax.all_to_all(split_up(value, dim, length), axis, 0, 0, tiled=True)  7.78 us
    ppermute x2, starting transfers between devices, shifted(): return lax.ppermute(block, axis, route)  6.42 us
    all_to_all x1, starting transfers between devices, per_device(): lax.all_to_all(result, ('seq', 'exp'), split_axis=0, concat_axis=0, tiled...  5.76 us
    dot_general x1, matrix products, expert_rows(): jnp.dot(activated, down_rows, preferred_element_type=jnp.float32)  5.45 us
  transfers between devices with their start and end apart: 6, of which 2 were waited for; matrix products, arithmetic and copies ran while one was open for 5% of the time, Pallas kernels for 0%

commit v1 on v0

v1 whole, which is shorter than its diff:
```python
import math

import jax
import jax.numpy as jnp
from jax import lax
from jax.experimental import pallas as pl
from jax.experimental.pallas import tpu as pltpu
from jax.sharding import PartitionSpec as P

MESH = pl.DeviceIdType.MESH
BF = jnp.bfloat16
F32 = jnp.float32
D = 2560
H = 1280
FF = 1440
COL = 256


def mm(a, b):
    return jnp.dot(a, b, preferred_element_type=F32)


def mm_nt(a, b):
    return lax.dot_general(a, b, (((1,), (1,)), ((), ())), preferred_element_type=F32)


def mm_tn(a, b):
    return lax.dot_general(a, b, (((0,), (0,)), ((), ())), preferred_element_type=F32)


def remote(src, dst, send_sem, recv_sem, device):
    return pltpu.make_async_remote_copy(
        src, dst, send_sem, recv_sem, device_id=device, device_id_type=MESH
    )


def aligned(value, multiple):
    return pl.multiple_of(value, multiple)


def loop(low, high, body):
    def step(i, carry):
        body(i)
        return carry

    lax.fori_loop(low, high, step, 0)


def layer_kernel(
    q_hbm, k_hbm, v_hbm, sink_ref, wo_hbm, res_hbm, gain_ref, ids_ref, gates_ref, wgu_hbm, wd_hbm,
    out_ref,
    q, kraw, vraw, wo, res, wgu, wd,
    kext, bdk, bdv, att,
    part_a, part_b, recv_z, recv_x, sum_a, sum_b, recv_a2, recv_b2,
    hidden, normed, dsel, wsel, perm,
    da1, db1, ra1, rb1, da2, db2, ra2, rb2, xb,
    both, act,
    ta1, yb, tb1, ua1, ub1, ta2, tb2, ua2, ub2,
    load_sem, kv_send, kv_recv, z_send, z_recv, x_send, x_recv, a2_send, a2_recv, b2_send, b2_recv,
    ex_send, ex_recv, sq_send, sq_recv,
):
    s = lax.axis_index("seq")
    e = lax.axis_index("exp")
    z = e // 4
    x = lax.rem(e, 4)
    parity = lax.rem(e, 2)
    mate = e + 1 - 2 * parity
    s_next = lax.rem(s + 1, 8)
    s_last = lax.rem(s + 7, 8)

    loads = [
        pltpu.make_async_copy(a, b, load_sem.at[i])
        for i, (a, b) in enumerate(
            [(k_hbm, kraw), (v_hbm, vraw), (q_hbm, q), (wo_hbm, wo), (res_hbm, res), (wgu_hbm, wgu), (wd_hbm, wd)]
        )
    ]
    for c in loads:
        c.start()

    barrier = pltpu.get_barrier_semaphore()

    def greet(device):
        pl.semaphore_signal(barrier, inc=1, device_id=device, device_id_type=MESH)

    loop(1, 16, lambda d: greet((s, lax.rem(e + d, 16))))
    loop(1, 8, lambda d: greet((lax.rem(s + d, 8), e)))
    greet((s_next, mate))
    greet((s_last, mate))

    eye = (
        lax.broadcasted_iota(jnp.int32, (32, 32), 0) == lax.broadcasted_iota(jnp.int32, (32, 32), 1)
    ).astype(F32).astype(BF)
    loads[0].wait()
    kext[parity, 0:32, 128:640] = mm_nt(eye, kraw[...]).astype(BF)
    loads[1].wait()
    kext[parity, 32:64, 128:640] = mm_nt(eye, vraw[...]).astype(BF)
    pl.semaphore_wait(barrier, 24)
    own_rows = kext.at[parity, :, pl.ds(128, 512)]
    own_tail = kext.at[parity, :, pl.ds(512, 128)]
    prior = kext.at[parity, :, pl.ds(0, 128)]
    kv_copies = [
        remote(own_rows, own_rows, kv_send.at[0], kv_recv.at[0], (s, mate)),
        remote(own_tail, prior, kv_send.at[1], kv_recv.at[1], (s_next, e)),
        remote(own_tail, prior, kv_send.at[2], kv_recv.at[2], (s_next, mate)),
    ]
    for c in kv_copies:
        c.start()

    ids = ids_ref[...]
    gates = gates_ref[...]
    before = (
        lax.broadcasted_iota(jnp.int32, (32, 32), 1) < lax.broadcasted_iota(jnp.int32, (32, 32), 0)
    ).astype(F32).astype(BF)
    lane = lax.broadcasted_iota(jnp.int32, (32, 256), 1)
    slot = (lane & 1).astype(F32)
    for order in range(2):
        expert = ((lane & 15) >> 1) * 16 + (lane >> 4) if order == 0 else lane >> 1
        named = jnp.zeros((32, 256), F32)
        weight = jnp.zeros((32, 256), F32)
        for k in range(4):
            same = ids[:, k : k + 1] == expert
            named = named + jnp.where(same, 1.0, 0.0)
            weight = weight + jnp.where(same, gates[:, k : k + 1], 0.0)
        rank = mm(before, named.astype(BF))
        chosen = jnp.where(rank == slot, named, 0.0)
        dsel[order] = chosen.astype(BF)
        weight = weight * chosen
        high = weight.astype(BF)
        wsel[order, 0:32, :] = high
        wsel[order, 32:64, :] = (weight - high.astype(F32)).astype(BF)
    row = lax.broadcasted_iota(jnp.int32, (256, 256), 0)
    col = lax.broadcasted_iota(jnp.int32, (256, 256), 1)
    to = ((row & 31) >> 1) * 16 + (row >> 5) * 2 + (row & 1)
    back = ((row & 15) >> 1) * 32 + (row >> 4) * 2 + (row & 1)
    perm[0] = jnp.where(col == to, 1.0, 0.0).astype(BF)
    perm[1] = jnp.where(col == back, 1.0, 0.0).astype(BF)

    bdk[...] = jnp.zeros((128, 512), BF)
    bdv[...] = jnp.zeros((128, 512), BF)
    loads[2].wait()
    loads[3].wait()
    for c in kv_copies:
        c.wait_recv()

    def z_copy(i):
        b = lax.rem(z + 1 + i, 4)
        return remote(part_a.at[b], recv_z.at[z], z_send.at[i], z_recv.at[i], (s, b * 4 + x))

    def x_copy(d, i):
        b = lax.rem(z + 1 + i, 4)
        other = lax.rem(x + 1 + d, 4)
        return remote(
            part_b.at[b, pl.ds(aligned(other * 32, 32), 32)],
            recv_x.at[x, b],
            x_send.at[d, i],
            x_recv.at[d, i],
            (s, z * 4 + other),
        )

    query_pos = lax.broadcasted_iota(jnp.int32, (128, 256), 0)
    key_pos = lax.broadcasted_iota(jnp.int32, (128, 256), 1)
    inside = (key_pos > query_pos) & (key_pos <= query_pos + 128)

    def attend(i):
        b = lax.rem(z + 1 + i, 4)
        window = pl.ds(aligned(b * 128, 128), 256)
        for half in range(2):
            for p in range(2):
                rows = slice(half * 64 + p * 32, half * 64 + p * 32 + 32)
                bdk[rows, half * 256 : half * 256 + 256] = kext[p, 0:32, window]
                bdv[rows, half * 256 : half * 256 + 256] = kext[p, 32:64, window]
        allowed = inside & (key_pos + (s * 512 + b * 128) >= 128)
        for pair in range(2):
            queries = q[pl.ds(aligned(b * 128, 128), 128), pair * 128 : pair * 128 + 128]
            scores = mm(queries, bdk[...]) * (1.0 / math.sqrt(64))
            probs = []
            for half in range(2):
                sink = sink_ref[pair * 2 + half]
                part = jnp.where(allowed, scores[:, half * 256 : half * 256 + 256], -1e30)
                highest = jnp.maximum(jnp.max(part, axis=1, keepdims=True), sink)
                raised = jnp.exp(part - highest)
                total = jnp.sum(raised, axis=1, keepdims=True) + jnp.exp(sink - highest)
                probs.append((raised * (1.0 / total)).astype(BF))
            mixed = mm_nt(jnp.concatenate(probs, axis=1), bdv[...])
            att[:, pair * 128 : pair * 128 + 128] = mixed.astype(BF)
        attended = att[...]
        for n in range(5):
            part_a[b, :, n * COL : n * COL + COL] = mm(attended, wo[:, n * COL : n * COL + COL]).astype(BF)

        @pl.when(i < 3)
        def _():
            z_copy(i).start()

        for n in range(5):
            part_b[b, :, n * COL : n * COL + COL] = mm(
                attended, wo[:, H + n * COL : H + n * COL + COL]
            ).astype(BF)
        for d in range(3):
            x_copy(d, i).start()

    loop(0, 4, attend)

    def a2_copy(i):
        other = lax.rem(x + 1 + i, 4)
        return remote(
            sum_a.at[pl.ds(aligned(other * 32, 32), 32)],
            recv_a2.at[x],
            a2_send.at[i],
            a2_recv.at[i],
            (s, z * 4 + other),
        )

    def b2_copy(i):
        b = lax.rem(z + 1 + i, 4)
        return remote(sum_b.at[b], recv_b2.at[z], b2_send.at[i], b2_recv.at[i], (s, b * 4 + x))

    for i in range(3):
        z_copy(i).wait_recv()

    def sum_over_z(i):
        other = lax.rem(x + 1 + i, 4)
        rows = pl.ds(aligned(other * 32, 32), 32)
        total = part_a[z, rows, :].astype(F32)
        for d in range(1, 4):
            total = total + recv_z[lax.rem(z + d, 4), rows, :].astype(F32)
        sum_a[rows, :] = total.astype(BF)

        @pl.when(i < 3)
        def _():
            a2_copy(i).start()

    loop(0, 4, sum_over_z)

    def sum_over_x(i):
        b = lax.rem(z + 1 + i, 4)
        for d in range(3):
            x_copy(d, i).wait_recv()
        total = part_b[b, pl.ds(aligned(x * 32, 32), 32), :].astype(F32)
        for d in range(1, 4):
            total = total + recv_x[lax.rem(x + d, 4), b].astype(F32)
        sum_b[b] = total.astype(BF)

        @pl.when(i < 3)
        def _():
            b2_copy(i).start()

    loop(0, 4, sum_over_x)

    loads[4].wait()
    for i in range(3):
        a2_copy(i).wait_recv()
    total = sum_a[pl.ds(aligned(x * 32, 32), 32), :].astype(F32)
    for d in range(1, 4):
        total = total + recv_a2[lax.rem(x + d, 4)].astype(F32)
    hidden_a = res[:, 0:H].astype(F32) + total
    hidden[:, 0:H] = hidden_a
    for i in range(3):
        b2_copy(i).wait_recv()
    total = sum_b[z].astype(F32)
    for d in range(1, 4):
        total = total + recv_b2[lax.rem(z + d, 4)].astype(F32)
    hidden_b = res[:, H:D].astype(F32) + total
    hidden[:, H:D] = hidden_b
    squares = jnp.sum(hidden_a * hidden_a, axis=1, keepdims=True) + jnp.sum(
        hidden_b * hidden_b, axis=1, keepdims=True
    )
    scale = lax.rsqrt(squares * (1.0 / D) + 1e-05)
    normed[:, 0:H] = (hidden[:, 0:H] * scale * gain_ref[:, 0:H]).astype(BF)
    normed[:, H:D] = (hidden[:, H:D] * scale * gain_ref[:, H:D]).astype(BF)

    def ex_copy(use, src, dst, d):
        g = lax.rem(e + d, 16)
        return remote(
            src.at[pl.ds(aligned(g * 16, 16), 16)],
            dst.at[pl.ds(aligned(e * 16, 16), 16)],
            ex_send.at[use, d - 1],
            ex_recv.at[use, d - 1],
            (s, g),
        )

    def sq_copy(use, src, dst, d):
        g = lax.rem(s + d, 8)
        return remote(
            src.at[pl.ds(aligned(g * 32, 32), 32)],
            dst.at[pl.ds(aligned(s * 32, 32), 32)],
            sq_send.at[use, d - 1],
            sq_recv.at[use, d - 1],
            (g, e),
        )

    def ex_start(use, src, dst):
        loop(1, 16, lambda d: ex_copy(use, src, dst, d).start())
        own = pl.ds(aligned(e * 16, 16), 16)
        dst[own, :] = src[own, :]

    def ex_wait(use, src, dst):
        loop(1, 16, lambda d: ex_copy(use, src, dst, d).wait_recv())

    def sq_start(use, src, dst):
        loop(1, 8, lambda d: sq_copy(use, src, dst, d).start())
        own = pl.ds(aligned(s * 32, 32), 32)
        dst[own, :] = src[own, :]

    def sq_wait(use, src, dst):
        loop(1, 8, lambda d: sq_copy(use, src, dst, d).wait_recv())

    def chunk(n, base=0):
        return pl.ds(aligned(base + n * COL, COL), COL)

    def permute(which, src, dst):
        def step(n):
            dst[:, chunk(n)] = mm(perm[which], src[:, chunk(n)]).astype(BF)

        loop(0, 5, step)

    def place_a(n):
        da1[:, chunk(n)] = mm_tn(dsel[0], normed[:, chunk(n)]).astype(BF)

    def place_b(n):
        db1[:, chunk(n)] = mm_tn(dsel[1], normed[:, chunk(n, H)]).astype(BF)

    loop(0, 5, place_a)
    ex_start(0, da1, ra1)
    loop(0, 5, place_b)
    sq_start(0, db1, rb1)
    ex_wait(0, da1, ra1)
    permute(0, ra1, da2)
    sq_start(1, da2, ra2)
    sq_wait(0, db1, rb1)
    permute(1, rb1, db2)
    ex_start(1, db2, rb2)
    sq_wait(1, da2, ra2)
    ex_wait(1, db2, rb2)
    permute(0, rb2, xb)

    loads[5].wait()

    def up(n):
        both[:, chunk(n)] = mm(ra2[...], wgu[0, 0:H, chunk(n)]) + mm(xb[...], wgu[0, H:D, chunk(n)])

    loop(0, 11, up)
    both[:, 2816:2880] = mm(ra2[...], wgu[0, 0:H, 2816:2880]) + mm(xb[...], wgu[0, H:D, 2816:2880])

    def activate(r):
        rows = pl.ds(aligned(r * 32, 32), 32)
        gate = both[rows, 0:FF]
        lift = both[rows, FF : 2 * FF]
        act[rows, :] = (gate * (1.0 / (1.0 + jnp.exp(-1.702 * gate))) * (lift + 1.0)).astype(BF)

    loop(0, 8, activate)
    loads[6].wait()

    def down_a(n):
        ta1[:, chunk(n)] = mm(act[...], wd[0, :, chunk(n)]).astype(BF)

    def down_b(n):
        yb[:, chunk(n)] = mm(act[...], wd[0, :, chunk(n, H)]).astype(BF)

    loop(0, 5, down_a)
    sq_start(2, ta1, ua1)
    loop(0, 5, down_b)
    permute(1, yb, tb1)
    ex_start(2, tb1, ub1)
    sq_wait(2, ta1, ua1)
    permute(1, ua1, ta2)
    ex_start(3, ta2, ua2)
    ex_wait(2, tb1, ub1)
    permute(0, ub1, tb2)
    sq_start(3, tb2, ub2)

    def combine(order, src, base, n):
        weighted = mm(wsel[order], src[:, chunk(n)])
        out_ref[:, chunk(n, base)] = (hidden[:, chunk(n, base)] + weighted[0:32] + weighted[32:64]).astype(BF)

    ex_wait(3, ta2, ua2)
    loop(0, 5, lambda n: combine(0, ua2, 0, n))
    sq_wait(3, tb2, ub2)
    loop(0, 5, lambda n: combine(1, ub2, H, n))

    for c in kv_copies:
        c.wait_send()
    for i in range(3):
        z_copy(i).wait_send()
        a2_copy(i).wait_send()
        b2_copy(i).wait_send()
        loop(0, 4, lambda j: x_copy(i, j).wait_send())
    for use, src, dst in ((0, da1, ra1), (1, db2, rb2), (2, tb1, ub1), (3, ta2, ua2)):
        loop(1, 16, lambda d: ex_copy(use, src, dst, d).wait_send())
    for use, src, dst in ((0, db1, rb1), (1, da2, ra2), (2, ta1, ua1), (3, tb2, ub2)):
        loop(1, 8, lambda d: sq_copy(use, src, dst, d).wait_send())


def per_device(
    queries, key_rows, value_rows, sink_logits, out_proj, residual, norm_gain, expert_ids, gate_weights,
    w_gate_up, w_down,
):
    hbm = pl.BlockSpec(memory_space=pl.ANY)
    vmem = pl.BlockSpec(memory_space=pltpu.VMEM)
    smem = pl.BlockSpec(memory_space=pltpu.SMEM)
    dma = pltpu.SemaphoreType.DMA
    wide = pltpu.VMEM((256, H), BF)
    scratch = [
        pltpu.VMEM((512, 256), BF),
        pltpu.VMEM((512, 32), BF),
        pltpu.VMEM((512, 32), BF),
        pltpu.VMEM((256, D), BF),
        pltpu.VMEM((32, D), BF),
        pltpu.VMEM((1, D, 2 * FF), BF),
        pltpu.VMEM((1, FF, D), BF),
        pltpu.VMEM((2, 64, 640), BF),
        pltpu.VMEM((128, 512), BF),
        pltpu.VMEM((128, 512), BF),
        pltpu.VMEM((128, 256), BF),
        pltpu.VMEM((4, 128, H), BF),
        pltpu.VMEM((4, 128, H), BF),
        pltpu.VMEM((4, 128, H), BF),
        pltpu.VMEM((4, 4, 32, H), BF),
        pltpu.VMEM((128, H), BF),
        pltpu.VMEM((4, 32, H), BF),
        pltpu.VMEM((4, 32, H), BF),
        pltpu.VMEM((4, 32, H), BF),
        pltpu.VMEM((32, D), F32),
        pltpu.VMEM((32, D), BF),
        pltpu.VMEM((2, 32, 256), BF),
        pltpu.VMEM((2, 64, 256), BF),
        pltpu.VMEM((2, 256, 256), BF),
        *[wide] * 9,
        pltpu.VMEM((256, 2 * FF), F32),
        pltpu.VMEM((256, FF), BF),
        *[wide] * 9,
        dma((7,)),
        dma((3,)),
        dma((3,)),
        dma((3,)),
        dma((3,)),
        dma((3, 4)),
        dma((3, 4)),
        dma((3,)),
        dma((3,)),
        dma((3,)),
        dma((3,)),
        dma((4, 15)),
        dma((4, 15)),
        dma((4, 7)),
        dma((4, 7)),
    ]
    return pl.pallas_call(
        layer_kernel,
        out_shape=jax.ShapeDtypeStruct((32, D), BF),
        in_specs=[hbm, hbm, hbm, smem, hbm, hbm, vmem, vmem, vmem, hbm, hbm],
        out_specs=vmem,
        scratch_shapes=scratch,
        compiler_params=pltpu.CompilerParams(
            collective_id=1, has_side_effects=True, vmem_limit_bytes=60 * 1024 * 1024
        ),
        name="layer",
    )(
        queries, key_rows, value_rows, sink_logits, out_proj, residual, norm_gain.reshape(1, D),
        expert_ids, gate_weights, w_gate_up, w_down,
    )


def solution(mesh):
    return jax.shard_map(
        per_device,
        mesh=mesh,
        in_specs=(
            P("seq", "exp"),
            P("seq", "exp"),
            P("seq", "exp"),
            P("exp"),
            P("exp", None),
            P(("seq", "exp"), None),
            P(),
            P(("seq", "exp"), None),
            P(("seq", "exp"), None),
            P(("seq", "exp"), None, None),
            P(("seq", "exp"), None, None),
        ),
        out_specs=P(("seq", "exp"), None),
        check_vma=False,
    )
```

time: 149 us -> 127 us (0.85)
  Pallas kernels: 0 us -> 97.7 us
  waiting for transfers between devices: 59.8 us -> 0 us
  blocking collectives: 26.9 us -> 0 us
  starting transfers between devices: 22.1 us -> 0 us
  matrix products: 17.4 us -> 0 us
  local copies, waits for them, and re-layouts: 14.3 us -> 28.9 us
  other arithmetic: 7 us -> 0 us
    pallas_call x0 -> x1, Pallas kernels: none -> 97.7 us  [per_device(): pl.pallas_call(layer_kernel, out_shape=jax.ShapeDtypeStruct((32, D), BF),...]
    all_to_all x2 -> x0, waiting for transfers between devices: 59.7 us -> none  [the longest x1 38.6 us: sent_and_summed(): parts = lax.all_to_all(split_up(value, dim, length), axis, 0, 0, tiled=True)]
    unnamed x14 -> x6, local copies, waits for them, and re-layouts: 0.21 us -> 27.6 us
    all_to_all x1 -> x0, blocking collectives: 26.9 us -> none  [per_device(): lax.all_to_all(outgoing, ('seq', 'exp'), split_axis=0, concat_axis=0, til...]
    dot_general x6 -> x0, matrix products: 17.4 us -> none  [the longest x1 7.98 us: expert_rows(): both = jnp.dot(rows_in, gate_up, preferred_element_type=jnp.float32)]
    all_to_all x2 -> x0, starting transfers between devices: 13.5 us -> none  [the longest x1 7.78 us: sent_and_summed(): parts = lax.all_to_all(split_up(value, dim, length), axis, 0, 0, tiled=True)]
    ppermute x4 -> x0, starting transfers between devices: 8.54 us -> none  [the longest x2 6.42 us: shifted(): return lax.ppermute(block, axis, route)]
    reshape x5 -> x1, local copies, waits for them, and re-layouts: 8.52 us -> 1.31 us  [per_device(): norm_gain.reshape(1, D)]
  transfers between devices with their start and end apart: 6 -> 0, of which waited for: 2 -> 0; matrix products, arithmetic and copies ran while one was open for 5% -> 0% of each run, Pallas kernels for 0% -> 0%
where the time goes in v1:
time: 127 us
  Pallas kernels  97.7 us (77%)
  local copies, waits for them, and re-layouts  28.9 us (23%)
    pallas_call x1, Pallas kernels, per_device(): pl.pallas_call(layer_kernel, out_shape=jax.ShapeDtypeStruct((32, D), BF),...  97.7 us
    unnamed x6, local copies, waits for them, and re-layouts  27.6 us

profile of v1, /device:TPU:1, one launch (start us, length us, event | category | flops | bytes accessed | tf_op | source)
XLA Modules:
  0.0 126.6 jit_solution(15090142950837264675)
XLA Ops:
  0.0 1.3 %reshape.3.gain_ref = f32[1,2560]{1,0:T(1,128)} reshape(f32[2560]{0:T(1024)} %param.17) | data formatting | bytes 20480 | tf_op jit(solution)/shard_map/reshape | solution.py:458
  1.3 1.4 %copy.14.ids_ref = s32[32,4]{1,0:T(8,128)} copy(s32[32,4]{0,1:T(4,128)} %param.18) | data formatting | bytes 1024 | tf_op args[7]
  2.7 1.4 %copy.15.gates_ref = f32[32,4]{1,0:T(8,128)} copy(f32[32,4]{0,1:T(4,128)} %param.19) | data formatting | bytes 1024 | tf_op args[8]
  4.0 1.5 %copy.12.k_hbm = bf16[512,32]{1,0:T(8,128)(2,1)} copy(bf16[512,32]{0,1:T(8,128)(2,1)} %param.12) | data formatting | bytes 65536 | tf_op args[1]
  5.5 1.5 %copy.13.v_hbm = bf16[512,32]{1,0:T(8,128)(2,1)} copy(bf16[512,32]{0,1:T(8,128)(2,1)} %param.13) | data formatting | bytes 65536 | tf_op args[2]
  7.1 20.2 %copy.16.wgu_hbm = bf16[1,2560,2880]{2,1,0:T(8,128)(2,1)} copy(bf16[1,2560,2880]{1,2,0:T(8,128)(2,1)} %param.20) | data formatting | bytes 29491200 | tf_op args[9]
  27.3 97.7 %layer.1 = bf16[32,2560]{1,0:T(8,128)(2,1)} custom-call(bf16[512,256]{1,0:T(8,128)(2,1)} %q_hbm.1, bf16[512,32]{1,0:T(8,128)(2,1)} %copy.12.k_hbm, bf16[512,32]{1,0:T(8,128)(2,1)} %copy.13.v_hbm, f32[4]{0:T(128)} %sink_ref.1, bf16[256,2560]{1,0:T(8,128)(2,1)} %wo_hbm.1, bf16[32,2560]{1,0:T(8,128)(2,1)} %res_hbm.1, f32[1,2560]{1,0:T(1,128)} %reshape.3.gain_ref, ...), custom_call_target="tpu_custom_call" | custom-call | tf_op jit(solution)/shard_map/layer/pallas_call | solution.py:447
  125.0 1.6 %copy.18 = bf16[32,2560]{1,0:T(8,128)(2,1)} copy(bf16[32,2560]{1,0:T(8,128)(2,1)} %layer.1) | data formatting | bytes 327680

commit v2 on v1

--- a/solution.py
+++ b/solution.py
@@ -22,10 +22,6 @@
 
 def mm_nt(a, b):
     return lax.dot_general(a, b, (((1,), (1,)), ((), ())), preferred_element_type=F32)
-
-
-def mm_tn(a, b):
-    return lax.dot_general(a, b, (((0,), (0,)), ((), ())), preferred_element_type=F32)
 
 
 def remote(src, dst, send_sem, recv_sem, device):
@@ -54,7 +50,7 @@
     part_a, part_b, recv_z, recv_x, sum_a, sum_b, recv_a2, recv_b2,
     hidden, normed, dsel, wsel, perm,
     da1, db1, ra1, rb1, da2, db2, ra2, rb2, xb,
-    both, act,
+    act,
     ta1, yb, tb1, ua1, ub1, ta2, tb2, ua2, ub2,
     load_sem, kv_send, kv_recv, z_send, z_recv, x_send, x_recv, a2_send, a2_recv, b2_send, b2_recv,
     ex_send, ex_recv, sq_send, sq_recv,
@@ -87,13 +83,10 @@
     greet((s_next, mate))
     greet((s_last, mate))
 
-    eye = (
-        lax.broadcasted_iota(jnp.int32, (32, 32), 0) == lax.broadcasted_iota(jnp.int32, (32, 32), 1)
-    ).astype(F32).astype(BF)
     loads[0].wait()
-    kext[parity, 0:32, 128:640] = mm_nt(eye, kraw[...]).astype(BF)
+    kext[parity, 0:32, 128:640] = kraw[...]
     loads[1].wait()
-    kext[parity, 32:64, 128:640] = mm_nt(eye, vraw[...]).astype(BF)
+    kext[parity, 32:64, 128:640] = vraw[...]
     pl.semaphore_wait(barrier, 24)
     own_rows = kext.at[parity, :, pl.ds(128, 512)]
     own_tail = kext.at[parity, :, pl.ds(512, 128)]
@@ -109,22 +102,22 @@
     ids = ids_ref[...]
     gates = gates_ref[...]
     before = (
-        lax.broadcasted_iota(jnp.int32, (32, 32), 1) < lax.broadcasted_iota(jnp.int32, (32, 32), 0)
+        lax.broadcasted_iota(jnp.int32, (32, 32), 0) < lax.broadcasted_iota(jnp.int32, (32, 32), 1)
     ).astype(F32).astype(BF)
-    lane = lax.broadcasted_iota(jnp.int32, (32, 256), 1)
-    slot = (lane & 1).astype(F32)
+    place = lax.broadcasted_iota(jnp.int32, (256, 32), 0)
+    slot = (place & 1).astype(F32)
     for order in range(2):
-        expert = ((lane & 15) >> 1) * 16 + (lane >> 4) if order == 0 else lane >> 1
-        named = jnp.zeros((32, 256), F32)
-        weight = jnp.zeros((32, 256), F32)
+        expert = ((place & 15) >> 1) * 16 + (place >> 4) if order == 0 else place >> 1
+        named = jnp.zeros((256, 32), F32)
+        weight = jnp.zeros((256, 32), F32)
         for k in range(4):
-            same = ids[:, k : k + 1] == expert
+            same = ids[k : k + 1, :] == expert
             named = named + jnp.where(same, 1.0, 0.0)
-            weight = weight + jnp.where(same, gates[:, k : k + 1], 0.0)
-        rank = mm(before, named.astype(BF))
+            weight = weight + jnp.where(same, gates[k : k + 1, :], 0.0)
+        rank = mm(named.astype(BF), before)
         chosen = jnp.where(rank == slot, named, 0.0)
         dsel[order] = chosen.astype(BF)
-        weight = weight * chosen
+        weight = jnp.transpose(weight * chosen)
         high = weight.astype(BF)
         wsel[order, 0:32, :] = high
         wsel[order, 32:64, :] = (weight - high.astype(F32)).astype(BF)
@@ -265,8 +258,7 @@
         hidden_b * hidden_b, axis=1, keepdims=True
     )
     scale = lax.rsqrt(squares * (1.0 / D) + 1e-05)
-    normed[:, 0:H] = (hidden[:, 0:H] * scale * gain_ref[:, 0:H]).astype(BF)
-    normed[:, H:D] = (hidden[:, H:D] * scale * gain_ref[:, H:D]).astype(BF)
+    normed[...] = (hidden[...] * scale * gain_ref[...].reshape(1, D)).astype(BF)
 
     def ex_copy(use, src, dst, d):
         g = lax.rem(e + d, 16)
@@ -314,10 +306,10 @@
         loop(0, 5, step)
 
     def place_a(n):
-        da1[:, chunk(n)] = mm_tn(dsel[0], normed[:, chunk(n)]).astype(BF)
+        da1[:, chunk(n)] = mm(dsel[0], normed[:, chunk(n)]).astype(BF)
 
     def place_b(n):
-        db1[:, chunk(n)] = mm_tn(dsel[1], normed[:, chunk(n, H)]).astype(BF)
+        db1[:, chunk(n)] = mm(dsel[1], normed[:, chunk(n, H)]).astype(BF)
 
     loop(0, 5, place_a)
     ex_start(0, da1, ra1)
@@ -335,19 +327,20 @@
 
     loads[5].wait()
 
-    def up(n):
-        both[:, chunk(n)] = mm(ra2[...], wgu[0, 0:H, chunk(n)]) + mm(xb[...], wgu[0, H:D, chunk(n)])
-
-    loop(0, 11, up)
-    both[:, 2816:2880] = mm(ra2[...], wgu[0, 0:H, 2816:2880]) + mm(xb[...], wgu[0, H:D, 2816:2880])
-
-    def activate(r):
-        rows = pl.ds(aligned(r * 32, 32), 32)
-        gate = both[rows, 0:FF]
-        lift = both[rows, FF : 2 * FF]
-        act[rows, :] = (gate * (1.0 / (1.0 + jnp.exp(-1.702 * gate))) * (lift + 1.0)).astype(BF)
-
-    loop(0, 8, activate)
+    def up(n, width):
+        rows = pl.ds(aligned(n * width, 16), width)
+        lift_rows = pl.ds(aligned(FF + n * width, 16), width)
+        pieces = []
+        for r in (rows, lift_rows):
+            pieces.append(mm_nt(ra2[...], wgu[0, r, 0:H]) + mm_nt(xb[...], wgu[0, r, H:D]))
+        gate, lift = pieces
+        act[:, n * width : n * width + width] = (
+            gate * (1.0 / (1.0 + jnp.exp(-1.702 * gate))) * (lift + 1.0)
+        ).astype(BF)
+
+    for n in range(5):
+        up(n, 256)
+    up(8, 160)
     loads[6].wait()
 
     def down_a(n):
@@ -401,11 +394,11 @@
     wide = pltpu.VMEM((256, H), BF)
     scratch = [
         pltpu.VMEM((512, 256), BF),
-        pltpu.VMEM((512, 32), BF),
-        pltpu.VMEM((512, 32), BF),
+        pltpu.VMEM((32, 512), BF),
+        pltpu.VMEM((32, 512), BF),
         pltpu.VMEM((256, D), BF),
         pltpu.VMEM((32, D), BF),
-        pltpu.VMEM((1, D, 2 * FF), BF),
+        pltpu.VMEM((1, 2 * FF, D), BF),
         pltpu.VMEM((1, FF, D), BF),
         pltpu.VMEM((2, 64, 640), BF),
         pltpu.VMEM((128, 512), BF),
@@ -421,11 +414,10 @@
         pltpu.VMEM((4, 32, H), BF),
         pltpu.VMEM((32, D), F32),
         pltpu.VMEM((32, D), BF),
-        pltpu.VMEM((2, 32, 256), BF),
+        pltpu.VMEM((2, 256, 32), BF),
         pltpu.VMEM((2, 64, 256), BF),
         pltpu.VMEM((2, 256, 256), BF),
         *[wide] * 9,
-        pltpu.VMEM((256, 2 * FF), F32),
         pltpu.VMEM((256, FF), BF),
         *[wide] * 9,
         dma((7,)),
@@ -455,8 +447,8 @@
         ),
         name="layer",
     )(
-        queries, key_rows, value_rows, sink_logits, out_proj, residual, norm_gain.reshape(1, D),
-        expert_ids, gate_weights, w_gate_up, w_down,
+        queries, key_rows.T, value_rows.T, sink_logits, out_proj, residual, norm_gain,
+        expert_ids.T, gate_weights.T, jnp.swapaxes(w_gate_up, 1, 2), w_down,
     )
 
 

time: 127 us -> 95.8 us (0.75)
  local copies, waits for them, and re-layouts: 28.9 us -> 1.59 us
  Pallas kernels: 97.7 us -> 94 us
    unnamed x6 -> x1, local copies, waits for them, and re-layouts: 27.6 us -> 1.59 us
    pallas_call x1, Pallas kernels: 97.7 us -> 94 us  [per_device(): pl.pallas_call(layer_kernel, out_shape=jax.ShapeDtypeStruct((32, D), BF),...]
    reshape x1 -> x0, local copies, waits for them, and re-layouts: 1.31 us -> none  [per_device(): norm_gain.reshape(1, D)]
where the time goes in v2:
time: 95.8 us; the launch traced here: 95.6 us
  Pallas kernels  94 us (98%)
  local copies, waits for them, and re-layouts  1.59 us (2%)
    pallas_call x1, Pallas kernels, per_device(): pl.pallas_call(layer_kernel, out_shape=jax.ShapeDtypeStruct((32, D), BF),...  94 us

profile of v2, /device:TPU:1, one launch (start us, length us, event | category | flops | bytes accessed | tf_op | source)
XLA Modules:
  0.0 95.6 jit_solution(1662930481230793355)
XLA Ops:
  0.0 94.0 %layer.1 = bf16[32,2560]{1,0:T(8,128)(2,1)} custom-call(bf16[512,256]{1,0:T(8,128)(2,1)} %q_hbm.1, bf16[32,512]{1,0:T(8,128)(2,1)} %bitcast.6, bf16[32,512]{1,0:T(8,128)(2,1)} %bitcast.7, f32[4]{0:T(128)} %sink_ref.1, bf16[256,2560]{1,0:T(8,128)(2,1)} %wo_hbm.1, bf16[32,2560]{1,0:T(8,128)(2,1)} %res_hbm.1, f32[2560]{0:T(1024)} %gain_ref.1, s32[4,32]{1,0:T(4,128)} %bitcast.8, ...), custom_call_target="tpu_custom_call" | custom-call | tf_op jit(solution)/shard_map/layer/pallas_call | solution.py:439
  94.0 1.6 %copy.13 = bf16[32,2560]{1,0:T(8,128)(2,1)} copy(bf16[32,2560]{1,0:T(8,128)(2,1)} %layer.1) | data formatting | bytes 327680

commit v3 on v2

--- a/solution.py
+++ b/solution.py
@@ -14,6 +14,8 @@
 H = 1280
 FF = 1440
 COL = 256
+CHUNKS = 5
+CHUNK = 512
 
 
 def mm(a, b):
@@ -48,12 +50,10 @@
     q, kraw, vraw, wo, res, wgu, wd,
     kext, bdk, bdv, att,
     part_a, part_b, recv_z, recv_x, sum_a, sum_b, recv_a2, recv_b2,
-    hidden, normed, dsel, wsel, perm,
-    da1, db1, ra1, rb1, da2, db2, ra2, rb2, xb,
-    act,
-    ta1, yb, tb1, ua1, ub1, ta2, tb2, ua2, ub2,
+    hidden, metas, select, weigh,
+    tokens, slots, rows_in, acc_gate, acc_lift, act, rows_out, answers, partial, returned,
     load_sem, kv_send, kv_recv, z_send, z_recv, x_send, x_recv, a2_send, a2_recv, b2_send, b2_recv,
-    ex_send, ex_recv, sq_send, sq_recv,
+    meta_send, meta_recv, ex_send, ex_recv, sq_send, sq_recv,
 ):
     s = lax.axis_index("seq")
     e = lax.axis_index("exp")
@@ -99,34 +99,20 @@
     for c in kv_copies:
         c.start()
 
-    ids = ids_ref[...]
-    gates = gates_ref[...]
-    before = (
-        lax.broadcasted_iota(jnp.int32, (32, 32), 0) < lax.broadcasted_iota(jnp.int32, (32, 32), 1)
-    ).astype(F32).astype(BF)
-    place = lax.broadcasted_iota(jnp.int32, (256, 32), 0)
-    slot = (place & 1).astype(F32)
-    for order in range(2):
-        expert = ((place & 15) >> 1) * 16 + (place >> 4) if order == 0 else place >> 1
-        named = jnp.zeros((256, 32), F32)
-        weight = jnp.zeros((256, 32), F32)
-        for k in range(4):
-            same = ids[k : k + 1, :] == expert
-            named = named + jnp.where(same, 1.0, 0.0)
-            weight = weight + jnp.where(same, gates[k : k + 1, :], 0.0)
-        rank = mm(named.astype(BF), before)
-        chosen = jnp.where(rank == slot, named, 0.0)
-        dsel[order] = chosen.astype(BF)
-        weight = jnp.transpose(weight * chosen)
-        high = weight.astype(BF)
-        wsel[order, 0:32, :] = high
-        wsel[order, 32:64, :] = (weight - high.astype(F32)).astype(BF)
-    row = lax.broadcasted_iota(jnp.int32, (256, 256), 0)
-    col = lax.broadcasted_iota(jnp.int32, (256, 256), 1)
-    to = ((row & 31) >> 1) * 16 + (row >> 5) * 2 + (row & 1)
-    back = ((row & 15) >> 1) * 32 + (row >> 4) * 2 + (row & 1)
-    perm[0] = jnp.where(col == to, 1.0, 0.0).astype(BF)
-    perm[1] = jnp.where(col == back, 1.0, 0.0).astype(BF)
+    own_lanes = (
+        lax.broadcasted_iota(jnp.int32, (32, 256), 1)
+        == lax.broadcasted_iota(jnp.int32, (32, 256), 0) + s * 32
+    )
+    own_lanes = jnp.where(own_lanes, 1.0, 0.0)
+    for part, ref in ((slice(0, 4), ids_ref), (slice(4, 8), gates_ref)):
+        metas[s, part, :] = jnp.dot(
+            ref[...].astype(F32), own_lanes, preferred_element_type=F32, precision=lax.Precision.HIGHEST
+        )
+
+    def meta_copy(d):
+        return remote(metas.at[s], metas.at[s], meta_send.at[d - 1], meta_recv.at[d - 1], (lax.rem(s + d, 8), e))
+
+    loop(1, 8, lambda d: meta_copy(d).start())
 
     bdk[...] = jnp.zeros((128, 512), BF)
     bdv[...] = jnp.zeros((128, 512), BF)
@@ -193,6 +179,29 @@
 
     loop(0, 4, attend)
 
+    loop(1, 8, lambda d: meta_copy(d).wait_recv())
+    meta = metas[0]
+    for i in range(1, 8):
+        meta = meta + metas[i]
+    place = lax.broadcasted_iota(jnp.int32, (256, 256), 0)
+    token = lax.broadcasted_iota(jnp.int32, (256, 256), 1)
+    mine = ((place & 15) >> 1) == (token >> 5)
+    expert = ((place >> 4) + s * 16).astype(F32)
+    named = jnp.zeros((256, 256), F32)
+    weight = jnp.zeros((256, 256), F32)
+    for k in range(4):
+        same = mine & (meta[k : k + 1, :] == expert)
+        named = named + jnp.where(same, 1.0, 0.0)
+        weight = weight + jnp.where(same, meta[4 + k : 5 + k, :], 0.0)
+    before = jnp.where(place < token, 1.0, 0.0).astype(BF)
+    rank = mm(named.astype(BF), before)
+    chosen = jnp.where(rank == (place & 1).astype(F32), named, 0.0)
+    select[...] = chosen.astype(BF)
+    weight = jnp.transpose(weight * chosen)
+    high = weight.astype(BF)
+    weigh[0] = high
+    weigh[1] = (weight - high.astype(F32)).astype(BF)
+
     def a2_copy(i):
         other = lax.rem(x + 1 + i, 4)
         return remote(
@@ -258,117 +267,101 @@
         hidden_b * hidden_b, axis=1, keepdims=True
     )
     scale = lax.rsqrt(squares * (1.0 / D) + 1e-05)
-    normed[...] = (hidden[...] * scale * gain_ref[...].reshape(1, D)).astype(BF)
-
-    def ex_copy(use, src, dst, d):
-        g = lax.rem(e + d, 16)
+    gain = gain_ref[...].reshape(1, D)
+
+    own_block = pl.ds(aligned(s * 32, 32), 32)
+    own_slots = pl.ds(aligned(e * 16, 16), 16)
+
+    def sq_copy(use, c, d):
+        peer = lax.rem(s + d, 8)
+        src, dst, rows = (tokens, tokens, own_block)
+        if use == 1:
+            src, dst, rows = (partial, returned, pl.ds(aligned(peer * 32, 32), 32))
         return remote(
-            src.at[pl.ds(aligned(g * 16, 16), 16)],
-            dst.at[pl.ds(aligned(e * 16, 16), 16)],
-            ex_send.at[use, d - 1],
-            ex_recv.at[use, d - 1],
-            (s, g),
-        )
-
-    def sq_copy(use, src, dst, d):
-        g = lax.rem(s + d, 8)
+            src.at[c, rows], dst.at[c, own_block], sq_send.at[use, c, d - 1], sq_recv.at[use, c, d - 1], (peer, e)
+        )
+
+    def ex_copy(use, c, d):
+        peer = lax.rem(e + d, 16)
+        src, dst = (slots, rows_in) if use == 0 else (rows_out, answers)
         return remote(
-            src.at[pl.ds(aligned(g * 32, 32), 32)],
-            dst.at[pl.ds(aligned(s * 32, 32), 32)],
-            sq_send.at[use, d - 1],
-            sq_recv.at[use, d - 1],
-            (g, e),
-        )
-
-    def ex_start(use, src, dst):
-        loop(1, 16, lambda d: ex_copy(use, src, dst, d).start())
-        own = pl.ds(aligned(e * 16, 16), 16)
-        dst[own, :] = src[own, :]
-
-    def ex_wait(use, src, dst):
-        loop(1, 16, lambda d: ex_copy(use, src, dst, d).wait_recv())
-
-    def sq_start(use, src, dst):
-        loop(1, 8, lambda d: sq_copy(use, src, dst, d).start())
-        own = pl.ds(aligned(s * 32, 32), 32)
-        dst[own, :] = src[own, :]
-
-    def sq_wait(use, src, dst):
-        loop(1, 8, lambda d: sq_copy(use, src, dst, d).wait_recv())
-
-    def chunk(n, base=0):
-        return pl.ds(aligned(base + n * COL, COL), COL)
-
-    def permute(which, src, dst):
-        def step(n):
-            dst[:, chunk(n)] = mm(perm[which], src[:, chunk(n)]).astype(BF)
-
-        loop(0, 5, step)
-
-    def place_a(n):
-        da1[:, chunk(n)] = mm(dsel[0], normed[:, chunk(n)]).astype(BF)
-
-    def place_b(n):
-        db1[:, chunk(n)] = mm(dsel[1], normed[:, chunk(n, H)]).astype(BF)
-
-    loop(0, 5, place_a)
-    ex_start(0, da1, ra1)
-    loop(0, 5, place_b)
-    sq_start(0, db1, rb1)
-    ex_wait(0, da1, ra1)
-    permute(0, ra1, da2)
-    sq_start(1, da2, ra2)
-    sq_wait(0, db1, rb1)
-    permute(1, rb1, db2)
-    ex_start(1, db2, rb2)
-    sq_wait(1, da2, ra2)
-    ex_wait(1, db2, rb2)
-    permute(0, rb2, xb)
-
+            src.at[c, pl.ds(aligned(peer * 16, 16), 16)],
+            dst.at[c, own_slots],
+            ex_send.at[use, c, d - 1],
+            ex_recv.at[use, c, d - 1],
+            (s, peer),
+        )
+
+    def columns(c):
+        return slice(c * CHUNK, c * CHUNK + CHUNK)
+
+    for c in range(CHUNKS):
+        tokens[c, own_block, :] = (hidden[:, columns(c)] * scale * gain[:, columns(c)]).astype(BF)
+        loop(1, 8, lambda d: sq_copy(0, c, d).start())
+
+    def dispatch(c):
+        loop(1, 8, lambda d: sq_copy(0, c, d).wait_recv())
+        for n in (slice(0, COL), slice(COL, CHUNK)):
+            slots[c, :, n] = mm(select[...], tokens[c, :, n]).astype(BF)
+        loop(1, 16, lambda d: ex_copy(0, c, d).start())
+        rows_in[c, own_slots, :] = slots[c, own_slots, :]
+
+    def up_tile(c, low, width):
+        out = pl.ds(aligned(low, 128), width)
+        tiles = []
+        for base, acc in ((0, acc_gate), (FF, acc_lift)):
+            weights = wgu[0, pl.ds(aligned(base + low, 16), width), columns(c)]
+            tile = mm_nt(rows_in[c], weights)
+            if c > 0:
+                tile = tile + acc[:, out]
+            if c < CHUNKS - 1:
+                acc[:, out] = tile
+            tiles.append(tile)
+        if c == CHUNKS - 1:
+            gate, lift = tiles
+            act[:, out] = (gate * (1.0 / (1.0 + jnp.exp(-1.702 * gate))) * (lift + 1.0)).astype(BF)
+
+    def up(c):
+        loop(1, 16, lambda d: ex_copy(0, c, d).wait_recv())
+        loop(0, 5, lambda n: up_tile(c, n * COL, COL))
+        up_tile(c, 5 * COL, FF - 5 * COL)
+
+    dispatch(0)
+    dispatch(1)
     loads[5].wait()
-
-    def up(n, width):
-        rows = pl.ds(aligned(n * width, 16), width)
-        lift_rows = pl.ds(aligned(FF + n * width, 16), width)
-        pieces = []
-        for r in (rows, lift_rows):
-            pieces.append(mm_nt(ra2[...], wgu[0, r, 0:H]) + mm_nt(xb[...], wgu[0, r, H:D]))
-        gate, lift = pieces
-        act[:, n * width : n * width + width] = (
-            gate * (1.0 / (1.0 + jnp.exp(-1.702 * gate))) * (lift + 1.0)
-        ).astype(BF)
-
-    for n in range(5):
-        up(n, 256)
-    up(8, 160)
+    for c in range(CHUNKS):
+        up(c)
+        if c + 2 < CHUNKS:
+            dispatch(c + 2)
+
     loads[6].wait()
-
-    def down_a(n):
-        ta1[:, chunk(n)] = mm(act[...], wd[0, :, chunk(n)]).astype(BF)
-
-    def down_b(n):
-        yb[:, chunk(n)] = mm(act[...], wd[0, :, chunk(n, H)]).astype(BF)
-
-    loop(0, 5, down_a)
-    sq_start(2, ta1, ua1)
-    loop(0, 5, down_b)
-    permute(1, yb, tb1)
-    ex_start(2, tb1, ub1)
-    sq_wait(2, ta1, ua1)
-    permute(1, ua1, ta2)
-    ex_start(3, ta2, ua2)
-    ex_wait(2, tb1, ub1)
-    permute(0, ub1, tb2)
-    sq_start(3, tb2, ub2)
-
-    def combine(order, src, base, n):
-        weighted = mm(wsel[order], src[:, chunk(n)])
-        out_ref[:, chunk(n, base)] = (hidden[:, chunk(n, base)] + weighted[0:32] + weighted[32:64]).astype(BF)
-
-    ex_wait(3, ta2, ua2)
-    loop(0, 5, lambda n: combine(0, ua2, 0, n))
-    sq_wait(3, tb2, ub2)
-    loop(0, 5, lambda n: combine(1, ub2, H, n))
+    for c in range(CHUNKS):
+        for n in range(2):
+            low = c * CHUNK + n * COL
+            rows_out[c, :, n * COL : n * COL + COL] = mm(act[...], wd[0, :, low : low + COL]).astype(BF)
+        loop(1, 16, lambda d: ex_copy(1, c, d).start())
+        answers[c, own_slots, :] = rows_out[c, own_slots, :]
+
+    def combine(c):
+        loop(1, 16, lambda d: ex_copy(1, c, d).wait_recv())
+        for n in (slice(0, COL), slice(COL, CHUNK)):
+            partial[c, :, n] = (mm(weigh[0], answers[c, :, n]) + mm(weigh[1], answers[c, :, n])).astype(BF)
+        loop(1, 8, lambda d: sq_copy(1, c, d).start())
+        returned[c, own_block, :] = partial[c, own_block, :]
+
+    def finish(c):
+        loop(1, 8, lambda d: sq_copy(1, c, d).wait_recv())
+        total = hidden[:, columns(c)]
+        for i in range(8):
+            total = total + returned[c, i * 32 : i * 32 + 32, :].astype(F32)
+        out_ref[:, columns(c)] = total.astype(BF)
+
+    combine(0)
+    combine(1)
+    for c in range(CHUNKS):
+        if c + 2 < CHUNKS:
+            combine(c + 2)
+        finish(c)
 
     for c in kv_copies:
         c.wait_send()
@@ -377,10 +370,11 @@
         a2_copy(i).wait_send()
         b2_copy(i).wait_send()
         loop(0, 4, lambda j: x_copy(i, j).wait_send())
-    for use, src, dst in ((0, da1, ra1), (1, db2, rb2), (2, tb1, ub1), (3, ta2, ua2)):
-        loop(1, 16, lambda d: ex_copy(use, src, dst, d).wait_send())
-    for use, src, dst in ((0, db1, rb1), (1, da2, ra2), (2, ta1, ua1), (3, tb2, ub2)):
-        loop(1, 8, lambda d: sq_copy(use, src, dst, d).wait_send())
+    loop(1, 8, lambda d: meta_copy(d).wait_send())
+    for use in range(2):
+        for c in range(CHUNKS):
+            loop(1, 16, lambda d: ex_copy(use, c, d).wait_send())
+            loop(1, 8, lambda d: sq_copy(use, c, d).wait_send())
 
 
 def per_device(
@@ -391,7 +385,7 @@
     vmem = pl.BlockSpec(memory_space=pltpu.VMEM)
     smem = pl.BlockSpec(memory_space=pltpu.SMEM)
     dma = pltpu.SemaphoreType.DMA
-    wide = pltpu.VMEM((256, H), BF)
+    wide = pltpu.VMEM((CHUNKS, 256, CHUNK), BF)
     scratch = [
         pltpu.VMEM((512, 256), BF),
         pltpu.VMEM((32, 512), BF),
@@ -413,13 +407,19 @@
         pltpu.VMEM((4, 32, H), BF),
         pltpu.VMEM((4, 32, H), BF),
         pltpu.VMEM((32, D), F32),
-        pltpu.VMEM((32, D), BF),
-        pltpu.VMEM((2, 256, 32), BF),
-        pltpu.VMEM((2, 64, 256), BF),
+        pltpu.VMEM((8, 8, 256), F32),
+        pltpu.VMEM((256, 256), BF),
         pltpu.VMEM((2, 256, 256), BF),
-        *[wide] * 9,
+        wide,
+        wide,
+        wide,
+        pltpu.VMEM((256, FF), F32),
+        pltpu.VMEM((256, FF), F32),
         pltpu.VMEM((256, FF), BF),
-        *[wide] * 9,
+        wide,
+        wide,
+        wide,
+        wide,
         dma((7,)),
         dma((3,)),
         dma((3,)),
@@ -431,10 +431,12 @@
         dma((3,)),
         dma((3,)),
         dma((3,)),
-        dma((4, 15)),
-        dma((4, 15)),
-        dma((4, 7)),
-        dma((4, 7)),
+        dma((7,)),
+        dma((7,)),
+        dma((2, CHUNKS, 15)),
+        dma((2, CHUNKS, 15)),
+        dma((2, CHUNKS, 7)),
+        dma((2, CHUNKS, 7)),
     ]
     return pl.pallas_call(
         layer_kernel,

time: 95.8 us -> 101 us (1.054)
  Pallas kernels: 94 us -> 99.3 us
    pallas_call x1, Pallas kernels: 94 us -> 99.3 us  [per_device(): pl.pallas_call(layer_kernel, out_shape=jax.ShapeDtypeStruct((32, D), BF),...]
where the time goes in v3:
time: 101 us
  Pallas kernels  99.3 us (98%)
  local copies, waits for them, and re-layouts  1.59 us (2%)
    pallas_call x1, Pallas kernels, per_device(): pl.pallas_call(layer_kernel, out_shape=jax.ShapeDtypeStruct((32, D), BF),...  99.3 us

profile of v3, /device:TPU:1, one launch (start us, length us, event | category | flops | bytes accessed | tf_op | source)
XLA Modules:
  0.0 100.9 jit_solution(17723135415284828586)
XLA Ops:
  0.0 99.3 %layer.1 = bf16[32,2560]{1,0:T(8,128)(2,1)} custom-call(bf16[512,256]{1,0:T(8,128)(2,1)} %q_hbm.1, bf16[32,512]{1,0:T(8,128)(2,1)} %bitcast.6, bf16[32,512]{1,0:T(8,128)(2,1)} %bitcast.7, f32[4]{0:T(128)} %sink_ref.1, bf16[256,2560]{1,0:T(8,128)(2,1)} %wo_hbm.1, bf16[32,2560]{1,0:T(8,128)(2,1)} %res_hbm.1, f32[2560]{0:T(1024)} %gain_ref.1, s32[4,32]{1,0:T(4,128)} %bitcast.8, ...), custom_call_target="tpu_custom_call" | custom-call | tf_op jit(solution)/shard_map/layer/pallas_call | solution.py:441
  99.3 1.6 %copy.13 = bf16[32,2560]{1,0:T(8,128)(2,1)} copy(bf16[32,2560]{1,0:T(8,128)(2,1)} %layer.1) | data formatting | bytes 327680

commit v4 on v3

v4 whole, which is shorter than its diff:
```python
import math

import jax
import jax.numpy as jnp
from jax import lax
from jax.experimental import pallas as pl
from jax.experimental.pallas import tpu as pltpu
from jax.sharding import PartitionSpec as P

MESH = pl.DeviceIdType.MESH
BF = jnp.bfloat16
F32 = jnp.float32
D = 2560
FF = 1440
COL = 256
CHUNKS = 5
CHUNK = 512
EXTRA = 128


def mm(a, b):
    return jnp.dot(a, b, preferred_element_type=F32)


def mm_nt(a, b):
    return lax.dot_general(a, b, (((1,), (1,)), ((), ())), preferred_element_type=F32)


def remote(src, dst, send_sem, recv_sem, device):
    return pltpu.make_async_remote_copy(
        src, dst, send_sem, recv_sem, device_id=device, device_id_type=MESH
    )


def aligned(value, multiple):
    return pl.multiple_of(value, multiple)


def loop(low, high, body):
    def step(i, carry):
        body(i)
        return carry

    lax.fori_loop(low, high, step, 0)


def layer_kernel(
    q_hbm, k_hbm, v_hbm, sink_ref, wo_hbm, res_hbm, gain_ref, ids_ref, gates_ref, wgu_hbm, wd_hbm,
    out_ref,
    q, kraw, vraw, wo, res, wgu, wd,
    kext, bdk, bdv, att,
    shares, recv_z, recv_x, sum_a, sum_b, recv_a2, recv_b2,
    hidden, metas, select, weigh,
    tokens_first, tokens_last, slots_first, slots_last, rows_first, rows_last,
    acc_gate, acc_lift, act, rows_out, answers, partial, crossed, summed, returned,
    load_sem, kv_send, kv_recv, first_send, first_recv, second_send, second_recv,
    meta_send, meta_recv, ex_send, ex_recv, gather_send, gather_recv, relay_send, relay_recv, cross_send, cross_recv,
    home_send, home_recv,
):
    s = lax.axis_index("seq")
    e = lax.axis_index("exp")
    z = e // 4
    x = lax.rem(e, 4)
    parity = lax.rem(e, 2)
    mate = e + 1 - 2 * parity
    y = s // 2
    core = lax.rem(s, 2)
    twin = s + 1 - 2 * core
    s_next = lax.rem(s + 1, 8)
    s_last = lax.rem(s + 7, 8)

    loads = [
        pltpu.make_async_copy(a, b, load_sem.at[i])
        for i, (a, b) in enumerate(
            [(k_hbm, kraw), (v_hbm, vraw), (q_hbm, q), (wo_hbm, wo), (res_hbm, res), (wgu_hbm, wgu), (wd_hbm, wd)]
        )
    ]
    for c in loads:
        c.start()

    barrier = pltpu.get_barrier_semaphore()

    def greet(device):
        pl.semaphore_signal(barrier, inc=1, device_id=device, device_id_type=MESH)

    loop(1, 16, lambda d: greet((s, lax.rem(e + d, 16))))
    loop(1, 8, lambda d: greet((lax.rem(s + d, 8), e)))
    greet((s_next, mate))
    greet((s_last, mate))

    loads[0].wait()
    kext[parity, 0:32, 128:640] = kraw[...]
    loads[1].wait()
    kext[parity, 32:64, 128:640] = vraw[...]
    pl.semaphore_wait(barrier, 24)
    own_rows = kext.at[parity, :, pl.ds(128, 512)]
    own_tail = kext.at[parity, :, pl.ds(512, 128)]
    prior = kext.at[parity, :, pl.ds(0, 128)]
    kv_copies = [
        remote(own_rows, own_rows, kv_send.at[0], kv_recv.at[0], (s, mate)),
        remote(own_tail, prior, kv_send.at[1], kv_recv.at[1], (s_next, e)),
        remote(own_tail, prior, kv_send.at[2], kv_recv.at[2], (s_next, mate)),
    ]
    for c in kv_copies:
        c.start()

    own_lanes = (
        lax.broadcasted_iota(jnp.int32, (32, 256), 1)
        == lax.broadcasted_iota(jnp.int32, (32, 256), 0) + s * 32
    )
    own_lanes = jnp.where(own_lanes, 1.0, 0.0)
    for part, ref in ((slice(0, 4), ids_ref), (slice(4, 8), gates_ref)):
        metas[s, part, :] = jnp.dot(
            ref[...].astype(F32), own_lanes, preferred_element_type=F32, precision=lax.Precision.HIGHEST
        )

    def meta_copy(d):
        return remote(metas.at[s], metas.at[s], meta_send.at[d - 1], meta_recv.at[d - 1], (lax.rem(s + d, 8), e))

    loop(1, 8, lambda d: meta_copy(d).start())

    bdk[...] = jnp.zeros((128, 512), BF)
    bdv[...] = jnp.zeros((128, 512), BF)
    loads[2].wait()
    loads[3].wait()
    for c in kv_copies:
        c.wait_recv()

    query_pos = lax.broadcasted_iota(jnp.int32, (128, 256), 0)
    key_pos = lax.broadcasted_iota(jnp.int32, (128, 256), 1)
    inside = (key_pos > query_pos) & (key_pos <= query_pos + 128)

    def attend(b):
        window = pl.ds(aligned(b * 128, 128), 256)
        for half in range(2):
            for p in range(2):
                rows = slice(half * 64 + p * 32, half * 64 + p * 32 + 32)
                bdk[rows, half * 256 : half * 256 + 256] = kext[p, 0:32, window]
                bdv[rows, half * 256 : half * 256 + 256] = kext[p, 32:64, window]
        allowed = inside & (key_pos + (s * 512 + b * 128) >= 128)
        for pair in range(2):
            queries = q[pl.ds(aligned(b * 128, 128), 128), pair * 128 : pair * 128 + 128]
            scores = mm(queries, bdk[...]) * (1.0 / math.sqrt(64))
            probs = []
            for half in range(2):
                sink = sink_ref[pair * 2 + half]
                part = jnp.where(allowed, scores[:, half * 256 : half * 256 + 256], -1e30)
                highest = jnp.maximum(jnp.max(part, axis=1, keepdims=True), sink)
                raised = jnp.exp(part - highest)
                total = jnp.sum(raised, axis=1, keepdims=True) + jnp.exp(sink - highest)
                probs.append((raised * (1.0 / total)).astype(BF))
            mixed = mm_nt(jnp.concatenate(probs, axis=1), bdv[...])
            att[pl.ds(aligned(b * 128, 128), 128), pair * 128 : pair * 128 + 128] = mixed.astype(BF)

    loop(0, 4, attend)

    def columns(c):
        return slice(c * CHUNK, c * CHUNK + CHUNK)

    def project(c):
        for half in range(2):
            low = c * CHUNK + half * COL
            shares[c, half] = mm(att[...], wo[:, low : low + COL]).reshape(4, 128, COL).astype(BF)
            for i in range(3):
                first_copy(c, half, i).start()

    def z_peer(i):
        return lax.rem(z + 1 + i, 4)

    def x_peer(i):
        return lax.rem(x + 1 + i, 4)

    def rows_of(peer):
        return pl.ds(aligned(peer * 32, 32), 32)

    def first_copy(c, half, i):
        if half == 0:
            src, dst, peer = shares.at[c, 0, z_peer(i)], recv_z.at[c, z], z_peer(i) * 4 + x
        else:
            src, dst, peer = shares.at[c, 1, :, rows_of(x_peer(i))], recv_x.at[c, x], z * 4 + x_peer(i)
        return remote(src, dst, first_send.at[c, half, i], first_recv.at[c, half, i], (s, peer))

    def second_copy(c, half, i):
        if half == 0:
            src, dst, peer = sum_a.at[c, rows_of(x_peer(i))], recv_a2.at[c, x], z * 4 + x_peer(i)
        else:
            src, dst, peer = sum_b.at[c, z_peer(i)], recv_b2.at[c, z], z_peer(i) * 4 + x
        return remote(src, dst, second_send.at[c, half, i], second_recv.at[c, half, i], (s, peer))

    def sum_first(c):
        for i in range(3):
            first_copy(c, 0, i).wait_recv()
        total = shares[c, 0, z].astype(F32)
        for i in range(3):
            total = total + recv_z[c, z_peer(i)].astype(F32)
        sum_a[c] = total.astype(BF)
        for i in range(3):
            second_copy(c, 0, i).start()
        for i in range(3):
            first_copy(c, 1, i).wait_recv()
        total = shares[c, 1, :, rows_of(x), :].astype(F32)
        for i in range(3):
            total = total + recv_x[c, x_peer(i)].astype(F32)
        sum_b[c] = total.astype(BF)
        for i in range(3):
            second_copy(c, 1, i).start()

    own_block = pl.ds(aligned(s * 32, 32), 32)
    own_slots = pl.ds(aligned(e * 16, 16), 16)

    def along_y(k):
        return lax.rem(y + k, 4) * 2 + core

    def gather_copy(c, k):
        block = tokens(c).at[own_block]
        peer = twin if k == 0 else along_y(k)
        return remote(block, block, gather_send.at[c, k], gather_recv.at[c, k], (peer, e))

    def relay_copy(c, k):
        block = tokens(c).at[pl.ds(aligned(along_y(4 - k) * 32, 32), 32)]
        return remote(block, block, relay_send.at[c, k - 1], relay_recv.at[c, k - 1], (twin, e))

    def cross_copy(c):
        return remote(partial.at[c, :, 1 - core], crossed.at[c], cross_send.at[c], cross_recv.at[c], (twin, e))

    def home_copy(c, k):
        return remote(
            summed.at[c, lax.rem(y + k, 4)],
            returned.at[c, y],
            home_send.at[c, k - 1],
            home_recv.at[c, k - 1],
            (along_y(k), e),
        )

    def tokens(c):
        return tokens_last if c == CHUNKS - 1 else tokens_first.at[c]

    def slots(c):
        return slots_last if c == CHUNKS - 1 else slots_first.at[c]

    def rows_in(c):
        return rows_last if c == CHUNKS - 1 else rows_first.at[c]

    squares = []

    def sum_second(c):
        for half, sums, place, received, peers in (
            (0, sum_a, rows_of(x), recv_a2, x_peer),
            (1, sum_b, z, recv_b2, z_peer),
        ):
            for i in range(3):
                second_copy(c, half, i).wait_recv()
            low = c * CHUNK + half * COL
            total = res[:, low : low + COL].astype(F32) + sums[c, place].astype(F32)
            for i in range(3):
                total = total + received[c, peers(i)].astype(F32)
            hidden[:, low : low + COL] = total
            squares.append(jnp.sum(total * total, axis=1, keepdims=True))
            tokens(c)[own_block, half * COL : half * COL + COL] = (total * gain[:, low : low + COL]).astype(BF)
        if c == CHUNKS - 1:
            mean = sum(squares[1:], squares[0]) * (1.0 / D)
            rest = jnp.broadcast_to(lax.rsqrt(mean + 1e-05), (32, EXTRA))
            lane = lax.broadcasted_iota(jnp.int32, (32, EXTRA), 1)
            parts = jnp.zeros((32, EXTRA), F32)
            for i in range(3):
                rounded = rest.astype(BF).astype(F32)
                parts = jnp.where(lane == i, rounded, parts)
                rest = rest - rounded
            tokens(c)[own_block, CHUNK : CHUNK + EXTRA] = parts.astype(BF)
        for k in (1, 3, 2, 0):
            gather_copy(c, k).start()

    def ex_copy(use, c, d):
        peer = lax.rem(e + d, 16)
        src, dst = (slots(c), rows_in(c)) if use == 0 else (rows_out.at[c], answers.at[c])
        return remote(
            src.at[pl.ds(aligned(peer * 16, 16), 16)],
            dst.at[own_slots],
            ex_send.at[use, c, d - 1],
            ex_recv.at[use, c, d - 1],
            (s, peer),
        )

    def relay(c):
        for k in (1, 3, 2):
            gather_copy(c, k).wait_recv()
            relay_copy(c, k).start()

    def dispatch(c):
        gather_copy(c, 0).wait_recv()
        for k in (1, 3, 2):
            relay_copy(c, k).wait_recv()
        pieces = [slice(0, COL), slice(COL, CHUNK)]
        if c == CHUNKS - 1:
            pieces.append(slice(CHUNK, CHUNK + EXTRA))
        for n in pieces:
            slots(c)[:, n] = mm(select[...], tokens(c)[:, n]).astype(BF)
        loop(1, 16, lambda d: ex_copy(0, c, d).start())
        rows_in(c)[own_slots, :] = slots(c)[own_slots, :]

    def up_tile(c, low, width, scale):
        out = pl.ds(aligned(low, 128), width)
        tiles = []
        for base, acc in ((0, acc_gate), (FF, acc_lift)):
            weights = wgu[0, pl.ds(aligned(base + low, 16), width), columns(c)]
            tile = mm_nt(rows_in(c)[:, 0:CHUNK], weights)
            if c > 0:
                tile = tile + acc[:, out]
            if c < CHUNKS - 1:
                acc[:, out] = tile
            tiles.append(tile)
        if c == CHUNKS - 1:
            gate, lift = tiles[0] * scale, tiles[1] * scale
            act[:, out] = (gate * (1.0 / (1.0 + jnp.exp(-1.702 * gate))) * (lift + 1.0)).astype(BF)

    def up(c):
        loop(1, 16, lambda d: ex_copy(0, c, d).wait_recv())
        scale = None
        if c == CHUNKS - 1:
            scale = jnp.sum(rows_in(c)[:, CHUNK : CHUNK + EXTRA].astype(F32), axis=1, keepdims=True)
        for n in range(5):
            up_tile(c, n * COL, COL, scale)
        up_tile(c, 5 * COL, FF - 5 * COL, scale)

    project(0)
    project(1)
    loop(1, 8, lambda d: meta_copy(d).wait_recv())
    meta = metas[0]
    for i in range(1, 8):
        meta = meta + metas[i]
    place = lax.broadcasted_iota(jnp.int32, (256, 256), 0)
    token = lax.broadcasted_iota(jnp.int32, (256, 256), 1)
    mine = ((place & 15) >> 1) == (token >> 5)
    expert = ((place >> 4) + s * 16).astype(F32)
    named = jnp.zeros((256, 256), F32)
    weight = jnp.zeros((256, 256), F32)
    for k in range(4):
        same = mine & (meta[k : k + 1, :] == expert)
        named = named + jnp.where(same, 1.0, 0.0)
        weight = weight + jnp.where(same, meta[4 + k : 5 + k, :], 0.0)
    before = jnp.where(place < token, 1.0, 0.0).astype(BF)
    rank = mm(named.astype(BF), before)
    chosen = jnp.where(rank == (place & 1).astype(F32), named, 0.0)
    select[...] = chosen.astype(BF)
    weight = jnp.transpose(weight * chosen)
    high = weight.astype(BF)
    weigh[0] = high
    weigh[1] = (weight - high.astype(F32)).astype(BF)

    loads[4].wait()
    gain = gain_ref[...].reshape(1, D)
    for step in range(CHUNKS + 3):
        if step < CHUNKS:
            sum_first(step)
        if step + 2 < CHUNKS:
            project(step + 2)
        if 0 <= step - 1 < CHUNKS:
            sum_second(step - 1)
        if 0 <= step - 2 < CHUNKS:
            relay(step - 2)
        if 0 <= step - 3 < CHUNKS:
            dispatch(step - 3)
        if step == CHUNKS + 1:
            loads[5].wait()
            up(0)
    for c in range(1, CHUNKS):
        up(c)

    loads[6].wait()
    for c in range(CHUNKS):
        for n in range(2):
            low = c * CHUNK + n * COL
            rows_out[c, :, n * COL : n * COL + COL] = mm(act[...], wd[0, :, low : low + COL]).astype(BF)
        loop(1, 16, lambda d: ex_copy(1, c, d).start())
        answers[c, own_slots, :] = rows_out[c, own_slots, :]

    def combine(c):
        loop(1, 16, lambda d: ex_copy(1, c, d).wait_recv())
        for n in (slice(0, COL), slice(COL, CHUNK)):
            sums = mm(weigh[0], answers[c, :, n]) + mm(weigh[1], answers[c, :, n])
            partial[c, :, :, :, n] = sums.reshape(4, 2, 32, COL).astype(BF)
        cross_copy(c).start()

    def reduce(c):
        cross_copy(c).wait_recv()
        for i in range(4):
            summed[c, i] = (partial[c, i, core].astype(F32) + crossed[c, i].astype(F32)).astype(BF)
        for k in (1, 3, 2):
            home_copy(c, k).start()

    def finish(c):
        total = hidden[:, columns(c)] + summed[c, y].astype(F32)
        for k in range(1, 4):
            home_copy(c, k).wait_recv()
        for k in range(1, 4):
            total = total + returned[c, lax.rem(y + k, 4)].astype(F32)
        out_ref[:, columns(c)] = total.astype(BF)

    for c in kv_copies:
        c.wait_send()
    loop(1, 8, lambda d: meta_copy(d).wait_send())
    for c in range(CHUNKS):
        for half in range(2):
            for i in range(3):
                first_copy(c, half, i).wait_send()
                second_copy(c, half, i).wait_send()
        for k in range(4):
            gather_copy(c, k).wait_send()
        for k in range(1, 4):
            relay_copy(c, k).wait_send()
        loop(1, 16, lambda d: ex_copy(0, c, d).wait_send())

    combine(0)
    for c in range(1, CHUNKS):
        reduce(c - 1)
        combine(c)
    reduce(CHUNKS - 1)
    for c in range(CHUNKS):
        loop(1, 16, lambda d: ex_copy(1, c, d).wait_send())
        finish(c)

    for c in range(CHUNKS):
        cross_copy(c).wait_send()
        for k in range(1, 4):
            home_copy(c, k).wait_send()


def per_device(
    queries, key_rows, value_rows, sink_logits, out_proj, residual, norm_gain, expert_ids, gate_weights,
    w_gate_up, w_down,
):
    hbm = pl.BlockSpec(memory_space=pl.ANY)
    vmem = pl.BlockSpec(memory_space=pltpu.VMEM)
    smem = pl.BlockSpec(memory_space=pltpu.SMEM)
    dma = pltpu.SemaphoreType.DMA
    wide = pltpu.VMEM((CHUNKS, 256, CHUNK), BF)
    narrow = pltpu.VMEM((CHUNKS, 4, 32, CHUNK), BF)
    scratch = [
        pltpu.VMEM((512, 256), BF),
        pltpu.VMEM((32, 512), BF),
        pltpu.VMEM((32, 512), BF),
        pltpu.VMEM((256, D), BF),
        pltpu.VMEM((32, D), BF),
        pltpu.VMEM((1, 2 * FF, D), BF),
        pltpu.VMEM((1, FF, D), BF),
        pltpu.VMEM((2, 64, 640), BF),
        pltpu.VMEM((128, 512), BF),
        pltpu.VMEM((128, 512), BF),
        pltpu.VMEM((512, 256), BF),
        pltpu.VMEM((CHUNKS, 2, 4, 128, COL), BF),
        pltpu.VMEM((CHUNKS, 4, 128, COL), BF),
        pltpu.VMEM((CHUNKS, 4, 4, 32, COL), BF),
        pltpu.VMEM((CHUNKS, 128, COL), BF),
        pltpu.VMEM((CHUNKS, 4, 32, COL), BF),
        pltpu.VMEM((CHUNKS, 4, 32, COL), BF),
        pltpu.VMEM((CHUNKS, 4, 32, COL), BF),
        pltpu.VMEM((32, D), F32),
        pltpu.VMEM((8, 8, 256), F32),
        pltpu.VMEM((256, 256), BF),
        pltpu.VMEM((2, 256, 256), BF),
        *[pltpu.VMEM((CHUNKS - 1, 256, CHUNK), BF), pltpu.VMEM((256, CHUNK + EXTRA), BF)] * 3,
        pltpu.VMEM((256, FF), F32),
        pltpu.VMEM((256, FF), F32),
        pltpu.VMEM((256, FF), BF),
        wide,
        wide,
        pltpu.VMEM((CHUNKS, 4, 2, 32, CHUNK), BF),
        narrow,
        narrow,
        narrow,
        dma((7,)),
        dma((3,)),
        dma((3,)),
        *[dma((CHUNKS, 2, 3))] * 4,
        dma((7,)),
        dma((7,)),
        dma((2, CHUNKS, 15)),
        dma((2, CHUNKS, 15)),
        dma((CHUNKS, 4)),
        dma((CHUNKS, 4)),
        dma((CHUNKS, 3)),
        dma((CHUNKS, 3)),
        dma((CHUNKS,)),
        dma((CHUNKS,)),
        dma((CHUNKS, 3)),
        dma((CHUNKS, 3)),
    ]
    return pl.pallas_call(
        layer_kernel,
        out_shape=jax.ShapeDtypeStruct((32, D), BF),
        in_specs=[hbm, hbm, hbm, smem, hbm, hbm, vmem, vmem, vmem, hbm, hbm],
        out_specs=vmem,
        scratch_shapes=scratch,
        compiler_params=pltpu.CompilerParams(
            collective_id=1, has_side_effects=True, vmem_limit_bytes=60 * 1024 * 1024
        ),
        name="layer",
    )(
        queries, key_rows.T, value_rows.T, sink_logits, out_proj, residual, norm_gain,
        expert_ids.T, gate_weights.T, jnp.swapaxes(w_gate_up, 1, 2), w_down,
    )


def solution(mesh):
    return jax.shard_map(
        per_device,
        mesh=mesh,
        in_specs=(
            P("seq", "exp"),
            P("seq", "exp"),
            P("seq", "exp"),
            P("exp"),
            P("exp", None),
            P(("seq", "exp"), None),
            P(),
            P(("seq", "exp"), None),
            P(("seq", "exp"), None),
            P(("seq", "exp"), None, None),
            P(("seq", "exp"), None, None),
        ),
        out_specs=P(("seq", "exp"), None),
        check_vma=False,
    )
```

time: 101 us -> 85.9 us (0.85)
  Pallas kernels: 99.3 us -> 84.1 us
    pallas_call x1, Pallas kernels: 99.3 us -> 84.1 us  [per_device(): pl.pallas_call(layer_kernel, out_shape=jax.ShapeDtypeStruct((32, D), BF),...]
where the time goes in v4:
time: 85.9 us; the launch traced here: 85.7 us
  Pallas kernels  84.1 us (98%)
  local copies, waits for them, and re-layouts  1.59 us (2%)
    pallas_call x1, Pallas kernels, per_device(): pl.pallas_call(layer_kernel, out_shape=jax.ShapeDtypeStruct((32, D), BF),...  84.1 us

profile of v4, /device:TPU:1, one launch (start us, length us, event | category | flops | bytes accessed | tf_op | source)
XLA Modules:
  0.0 85.7 jit_solution(12235288478299155676)
XLA Ops:
  0.0 84.1 %layer.1 = bf16[32,2560]{1,0:T(8,128)(2,1)} custom-call(bf16[512,256]{1,0:T(8,128)(2,1)} %q_hbm.1, bf16[32,512]{1,0:T(8,128)(2,1)} %bitcast.6, bf16[32,512]{1,0:T(8,128)(2,1)} %bitcast.7, f32[4]{0:T(128)} %sink_ref.1, bf16[256,2560]{1,0:T(8,128)(2,1)} %wo_hbm.1, bf16[32,2560]{1,0:T(8,128)(2,1)} %res_hbm.1, f32[2560]{0:T(1024)} %gain_ref.1, s32[4,32]{1,0:T(4,128)} %bitcast.8, ...), custom_call_target="tpu_custom_call" | custom-call | tf_op jit(solution)/shard_map/layer/pallas_call | solution.py:488
  84.1 1.6 %copy.13 = bf16[32,2560]{1,0:T(8,128)(2,1)} copy(bf16[32,2560]{1,0:T(8,128)(2,1)} %layer.1) | data formatting | bytes 327680

commit v5 on v4

v5 whole, which is shorter than its diff:
```python
import math

import jax
import jax.numpy as jnp
from jax import lax
from jax.experimental import pallas as pl
from jax.experimental.pallas import tpu as pltpu
from jax.sharding import PartitionSpec as P

MESH = pl.DeviceIdType.MESH
BF = jnp.bfloat16
F32 = jnp.float32
D = 2560
FF = 1440
COL = 256
EXTRA = 128
WIDTHS = (512, 512, 768, 512, 256)
BACK = (256, 768, 768, 512, 256)
CHUNKS = len(WIDTHS)


def mm(a, b):
    return jnp.dot(a, b, preferred_element_type=F32)


def mm_nt(a, b):
    return lax.dot_general(a, b, (((1,), (1,)), ((), ())), preferred_element_type=F32)


def remote(src, dst, send_sem, recv_sem, device):
    return pltpu.make_async_remote_copy(
        src, dst, send_sem, recv_sem, device_id=device, device_id_type=MESH
    )


def aligned(value, multiple):
    return pl.multiple_of(value, multiple)


def arrived(parts, sem):
    pltpu.make_async_copy(parts, parts, sem).wait()


def loop(low, high, body):
    def step(i, carry):
        body(i)
        return carry

    lax.fori_loop(low, high, step, 0)


def layer_kernel(
    q_hbm, k_hbm, v_hbm, sink_ref, wo_hbm, res_hbm, gain_hbm, ids_hbm, gates_hbm, wgu_hbm, wd_hbm, out_ref, *scratch
):
    take = iter(scratch)

    def per_chunk():
        return [next(take) for _ in range(CHUNKS)]

    q, kraw, vraw, wo, res, wgu, wd, gain_ref, ids_ref, gates_ref = [next(take) for _ in range(10)]
    kext, bdk, bdv, att, hidden, metas, select, weigh, acc_gate, acc_lift, act = [next(take) for _ in range(11)]
    shares, recv_z, recv_x, sum_a, sum_b, recv_a2, recv_b2 = [per_chunk() for _ in range(7)]
    tokens, slots, rows_in = [per_chunk() for _ in range(3)]
    rows_out, answers, partial, crossed, summed, returned = [per_chunk() for _ in range(6)]
    load_sem, kv_send, kv_recv, first_send, first_recv, second_send, second_recv = [next(take) for _ in range(7)]
    meta_send, meta_recv, ex_send, ex_recv, gather_send, gather_recv = [next(take) for _ in range(6)]
    relay_send, relay_recv, cross_send, cross_recv, home_send, home_recv = [next(take) for _ in range(6)]
    s = lax.axis_index("seq")
    e = lax.axis_index("exp")
    z = e // 4
    x = lax.rem(e, 4)
    parity = lax.rem(e, 2)
    mate = e + 1 - 2 * parity
    y = s // 2
    core = lax.rem(s, 2)
    twin = s + 1 - 2 * core
    s_next = lax.rem(s + 1, 8)
    s_last = lax.rem(s + 7, 8)

    loads = [
        pltpu.make_async_copy(a, b, load_sem.at[i])
        for i, (a, b) in enumerate(
            [
                (k_hbm, kraw), (v_hbm, vraw), (q_hbm, q), (wo_hbm, wo), (res_hbm, res), (wgu_hbm, wgu), (wd_hbm, wd),
                (gain_hbm, gain_ref), (ids_hbm, ids_ref), (gates_hbm, gates_ref),
            ]
        )
    ]
    for i in (0, 1, 8, 9, 2, 3, 7, 4, 5, 6):
        loads[i].start()

    barrier = pltpu.get_barrier_semaphore()

    def greet(device):
        pl.semaphore_signal(barrier, inc=1, device_id=device, device_id_type=MESH)

    loop(1, 16, lambda d: greet((s, lax.rem(e + d, 16))))
    loop(1, 8, lambda d: greet((lax.rem(s + d, 8), e)))
    greet((s_next, mate))
    greet((s_last, mate))

    loads[0].wait()
    kext[parity, 0:32, 128:640] = kraw[...]
    loads[1].wait()
    kext[parity, 32:64, 128:640] = vraw[...]
    pl.semaphore_wait(barrier, 24)
    own_rows = kext.at[parity, :, pl.ds(128, 512)]
    own_tail = kext.at[parity, :, pl.ds(512, 128)]
    prior = kext.at[parity, :, pl.ds(0, 128)]
    kv_copies = [
        remote(own_rows, own_rows, kv_send.at[0], kv_recv.at[0], (s, mate)),
        remote(own_tail, prior, kv_send.at[1], kv_recv.at[1], (s_next, e)),
        remote(own_tail, prior, kv_send.at[2], kv_recv.at[2], (s_next, mate)),
    ]
    for c in kv_copies:
        c.start()

    own_lanes = (
        lax.broadcasted_iota(jnp.int32, (32, 256), 1)
        == lax.broadcasted_iota(jnp.int32, (32, 256), 0) + s * 32
    )
    own_lanes = jnp.where(own_lanes, 1.0, 0.0)
    loads[8].wait()
    loads[9].wait()
    for part, ref in ((slice(0, 4), ids_ref), (slice(4, 8), gates_ref)):
        metas[s, part, :] = jnp.dot(
            ref[...].astype(F32), own_lanes, preferred_element_type=F32, precision=lax.Precision.HIGHEST
        )

    def meta_copy(d):
        return remote(metas.at[s], metas.at[s], meta_send.at[0], meta_recv.at[0], (lax.rem(s + d, 8), e))

    loop(1, 8, lambda d: meta_copy(d).start())

    bdk[...] = jnp.zeros((4, 128, 512), BF)
    bdv[...] = jnp.zeros((4, 128, 512), BF)
    loads[2].wait()
    loads[3].wait()
    for c in kv_copies:
        c.wait_recv()

    query_pos = lax.broadcasted_iota(jnp.int32, (128, 256), 0)
    key_pos = lax.broadcasted_iota(jnp.int32, (128, 256), 1)
    inside = (key_pos > query_pos) & (key_pos <= query_pos + 128)

    def attend(b):
        window = pl.ds(aligned(b * 128, 128), 256)
        for half in range(2):
            for p in range(2):
                rows = slice(half * 64 + p * 32, half * 64 + p * 32 + 32)
                bdk[b, rows, half * 256 : half * 256 + 256] = kext[p, 0:32, window]
                bdv[b, rows, half * 256 : half * 256 + 256] = kext[p, 32:64, window]
        allowed = inside & (key_pos + (s * 512 + b * 128) >= 128)
        for pair in range(2):
            queries = q[pl.ds(aligned(b * 128, 128), 128), pair * 128 : pair * 128 + 128]
            scores = mm(queries, bdk[b]) * (1.0 / math.sqrt(64))
            probs = []
            for half in range(2):
                sink = sink_ref[pair * 2 + half]
                part = jnp.where(allowed, scores[:, half * 256 : half * 256 + 256], -1e30)
                highest = jnp.maximum(jnp.max(part, axis=1, keepdims=True), sink)
                raised = jnp.exp(part - highest)
                total = jnp.sum(raised, axis=1, keepdims=True) + jnp.exp(sink - highest)
                probs.append((raised * (1.0 / total)).astype(BF))
            mixed = mm_nt(jnp.concatenate(probs, axis=1), bdv[b])
            att[pl.ds(aligned(b * 128, 128), 128), pair * 128 : pair * 128 + 128] = mixed.astype(BF)

    for b in range(4):
        attend(b)

    def columns(c, widths=WIDTHS):
        return slice(sum(widths[:c]), sum(widths[: c + 1]))

    def tiles(width):
        return [slice(low, min(low + COL, width)) for low in range(0, width, COL)]

    def half_columns(c, half):
        wide = WIDTHS[c] // 2
        return slice(sum(WIDTHS[:c]) + half * wide, sum(WIDTHS[:c]) + half * wide + wide)

    def project(c):
        for half in range(2):
            share = mm(att[...], wo[:, half_columns(c, half)])
            shares[c][half] = share.reshape(4, 128, WIDTHS[c] // 2).astype(BF)
            for i in range(3):
                first_copy(c, half, i).start()

    def z_peer(i):
        return lax.rem(z + 1 + i, 4)

    def x_peer(i):
        return lax.rem(x + 1 + i, 4)

    def rows_of(peer):
        return pl.ds(aligned(peer * 32, 32), 32)

    def first_copy(c, half, i):
        if half == 0:
            src, dst, peer = shares[c].at[0, z_peer(i)], recv_z[c].at[z], z_peer(i) * 4 + x
        else:
            src, dst, peer = shares[c].at[1, :, rows_of(x_peer(i))], recv_x[c].at[x], z * 4 + x_peer(i)
        return remote(src, dst, first_send.at[c, half], first_recv.at[c, half], (s, peer))

    def second_copy(c, half, i):
        if half == 0:
            src, dst, peer = sum_a[c].at[rows_of(x_peer(i))], recv_a2[c].at[x], z * 4 + x_peer(i)
        else:
            src, dst, peer = sum_b[c].at[z_peer(i)], recv_b2[c].at[z], z_peer(i) * 4 + x
        return remote(src, dst, second_send.at[c, half], second_recv.at[c, half], (s, peer))

    def sum_first(c):
        arrived(recv_z[c].at[pl.ds(0, 3)], first_recv.at[c, 0])
        total = shares[c][0, z].astype(F32)
        for i in range(3):
            total = total + recv_z[c][z_peer(i)].astype(F32)
        sum_a[c][...] = total.astype(BF)
        for i in range(3):
            second_copy(c, 0, i).start()
        arrived(recv_x[c].at[pl.ds(0, 3)], first_recv.at[c, 1])
        total = shares[c][1, :, rows_of(x), :].astype(F32)
        for i in range(3):
            total = total + recv_x[c][x_peer(i)].astype(F32)
        sum_b[c][...] = total.astype(BF)
        for i in range(3):
            second_copy(c, 1, i).start()

    own_block = pl.ds(aligned(s * 32, 32), 32)
    own_slots = pl.ds(aligned(e * 16, 16), 16)

    def along_y(k):
        return lax.rem(y + k, 4) * 2 + core

    def gather_copy(c, k):
        block = tokens[c].at[own_block]
        peer = twin if k == 0 else along_y(k)
        return remote(block, block, gather_send.at[c], gather_recv.at[c, k], (peer, e))

    def relay_copy(c, k):
        block = tokens[c].at[pl.ds(aligned(along_y(4 - k) * 32, 32), 32)]
        return remote(block, block, relay_send.at[c], relay_recv.at[c], (twin, e))

    def cross_copy(c):
        return remote(partial[c].at[:, 1 - core], crossed[c], cross_send.at[c], cross_recv.at[c], (twin, e))

    def home_copy(c, k):
        return remote(
            summed[c].at[lax.rem(y + k, 4)],
            returned[c].at[y],
            home_send.at[c],
            home_recv.at[c],
            (along_y(k), e),
        )

    squares = []

    def sum_second(c):
        for half, sums, place, received, peers in (
            (0, sum_a, rows_of(x), recv_a2, x_peer),
            (1, sum_b, z, recv_b2, z_peer),
        ):
            arrived(received[c].at[pl.ds(0, 3)], second_recv.at[c, half])
            here = half_columns(c, half)
            wide = WIDTHS[c] // 2
            total = res[:, here].astype(F32) + sums[c][place].astype(F32)
            for i in range(3):
                total = total + received[c][peers(i)].astype(F32)
            hidden[:, here] = total
            squares.append(jnp.sum(total * total, axis=1, keepdims=True))
            tokens[c][own_block, half * wide : half * wide + wide] = (total * gain[:, here]).astype(BF)
        if c == CHUNKS - 1:
            mean = sum(squares[1:], squares[0]) * (1.0 / D)
            rest = jnp.broadcast_to(lax.rsqrt(mean + 1e-05), (32, EXTRA))
            lane = lax.broadcasted_iota(jnp.int32, (32, EXTRA), 1)
            parts = jnp.zeros((32, EXTRA), F32)
            for i in range(3):
                rounded = rest.astype(BF).astype(F32)
                parts = jnp.where(lane == i, rounded, parts)
                rest = rest - rounded
            tokens[c][own_block, WIDTHS[c] : WIDTHS[c] + EXTRA] = parts.astype(BF)
        for k in (1, 3, 2, 0):
            gather_copy(c, k).start()

    def ex_copy(use, c, d):
        peer = lax.rem(e + d, 16)
        src, dst = (slots[c], rows_in[c]) if use == 0 else (rows_out[c], answers[c])
        return remote(
            src.at[pl.ds(aligned(peer * 16, 16), 16)],
            dst.at[own_slots],
            ex_send.at[use, c],
            ex_recv.at[use, c],
            (s, peer),
        )

    def relay(c):
        for k in (1, 3, 2):
            gather_copy(c, k).wait_recv()
            relay_copy(c, k).start()

    def dispatch(c):
        gather_copy(c, 0).wait_recv()
        arrived(tokens[c].at[pl.ds(0, 96)], relay_recv.at[c])
        for n in tiles(WIDTHS[c] + (EXTRA if c == CHUNKS - 1 else 0)):
            slots[c][:, n] = mm(select[...], tokens[c][:, n]).astype(BF)
        loop(1, 16, lambda d: ex_copy(0, c, d).start())
        rows_in[c][own_slots, :] = slots[c][own_slots, :]

    def up_tile(c, low, width, scale):
        out = pl.ds(aligned(low, 128), width)
        sums = []
        for base, acc in ((0, acc_gate), (FF, acc_lift)):
            weights = wgu[0, pl.ds(aligned(base + low, 16), width), columns(c)]
            tile = mm_nt(rows_in[c][:, 0 : WIDTHS[c]], weights)
            if c > 0:
                tile = tile + acc[:, out]
            if c < CHUNKS - 1:
                acc[:, out] = tile
            sums.append(tile)
        if c == CHUNKS - 1:
            gate, lift = sums[0] * scale, sums[1] * scale
            act[:, out] = (gate * (1.0 / (1.0 + jnp.exp(-1.702 * gate))) * (lift + 1.0)).astype(BF)

    def up(c):
        arrived(rows_in[c].at[pl.ds(0, 240)], ex_recv.at[0, c])
        scale = None
        if c == CHUNKS - 1:
            scale = jnp.sum(rows_in[c][:, WIDTHS[c] : WIDTHS[c] + EXTRA].astype(F32), axis=1, keepdims=True)
        for n in range(5):
            up_tile(c, n * COL, COL, scale)
        up_tile(c, 5 * COL, FF - 5 * COL, scale)

    project(0)
    project(1)
    arrived(metas.at[pl.ds(0, 7)], meta_recv.at[0])
    meta = metas[0]
    for i in range(1, 8):
        meta = meta + metas[i]
    place = lax.broadcasted_iota(jnp.int32, (256, 256), 0)
    token = lax.broadcasted_iota(jnp.int32, (256, 256), 1)
    mine = ((place & 15) >> 1) == (token >> 5)
    expert = ((place >> 4) + s * 16).astype(F32)
    named = jnp.zeros((256, 256), F32)
    weight = jnp.zeros((256, 256), F32)
    for k in range(4):
        same = mine & (meta[k : k + 1, :] == expert)
        named = named + jnp.where(same, 1.0, 0.0)
        weight = weight + jnp.where(same, meta[4 + k : 5 + k, :], 0.0)
    before = jnp.where(place < token, 1.0, 0.0).astype(BF)
    rank = mm(named.astype(BF), before)
    chosen = jnp.where(rank == (place & 1).astype(F32), named, 0.0)
    select[...] = chosen.astype(BF)
    weight = jnp.transpose(weight * chosen)
    high = weight.astype(BF)
    weigh[0] = high
    weigh[1] = (weight - high.astype(F32)).astype(BF)

    loads[4].wait()
    loads[7].wait()
    gain = gain_ref[...].reshape(1, D)
    for c in range(CHUNKS):
        sum_first(c)
        if c + 2 < CHUNKS:
            project(c + 2)
        if c >= 1:
            sum_second(c - 1)
        if c >= 2:
            relay(c - 2)
        if c >= 3:
            dispatch(c - 3)
    sum_second(4)
    for c in range(3, CHUNKS):
        relay(c)
        dispatch(c - 1)
    dispatch(4)
    loads[5].wait()
    for c in range(CHUNKS):
        up(c)

    loads[6].wait()
    for c in range(CHUNKS):
        low = sum(BACK[:c])
        for n in tiles(BACK[c]):
            rows_out[c][:, n] = mm(act[...], wd[0, :, low + n.start : low + n.stop]).astype(BF)
        loop(1, 16, lambda d: ex_copy(1, c, d).start())
        answers[c][own_slots, :] = rows_out[c][own_slots, :]

    def combine(c):
        arrived(answers[c].at[pl.ds(0, 240)], ex_recv.at[1, c])
        for n in tiles(BACK[c]):
            sums = mm(weigh[0], answers[c][:, n]) + mm(weigh[1], answers[c][:, n])
            partial[c][:, :, :, n] = sums.reshape(4, 2, 32, n.stop - n.start).astype(BF)
        cross_copy(c).start()

    def reduce(c):
        cross_copy(c).wait_recv()
        for i in range(4):
            summed[c][i] = (partial[c][i, core].astype(F32) + crossed[c][i].astype(F32)).astype(BF)
        for k in (1, 3, 2):
            home_copy(c, k).start()

    def finish(c):
        total = hidden[:, columns(c, BACK)] + summed[c][y].astype(F32)
        arrived(returned[c].at[pl.ds(0, 3)], home_recv.at[c])
        for k in range(1, 4):
            total = total + returned[c][lax.rem(y + k, 4)].astype(F32)
        out_ref[:, columns(c, BACK)] = total.astype(BF)

    for c in kv_copies:
        c.wait_send()
    arrived(metas.at[pl.ds(0, 7)], meta_send.at[0])
    for c in range(CHUNKS):
        arrived(recv_z[c].at[pl.ds(0, 3)], first_send.at[c, 0])
        arrived(recv_x[c].at[pl.ds(0, 3)], first_send.at[c, 1])
        arrived(recv_a2[c].at[pl.ds(0, 3)], second_send.at[c, 0])
        arrived(recv_b2[c].at[pl.ds(0, 3)], second_send.at[c, 1])
        arrived(tokens[c].at[pl.ds(0, 128)], gather_send.at[c])
        arrived(tokens[c].at[pl.ds(0, 96)], relay_send.at[c])
        arrived(slots[c].at[pl.ds(0, 240)], ex_send.at[0, c])

    combine(0)
    for c in range(1, CHUNKS):
        reduce(c - 1)
        combine(c)
    reduce(CHUNKS - 1)
    for c in range(CHUNKS):
        arrived(rows_out[c].at[pl.ds(0, 240)], ex_send.at[1, c])
        finish(c)

    for c in range(CHUNKS):
        cross_copy(c).wait_send()
        arrived(summed[c].at[pl.ds(0, 3)], home_send.at[c])


def per_device(
    queries, key_rows, value_rows, sink_logits, out_proj, residual, norm_gain, expert_ids, gate_weights,
    w_gate_up, w_down,
):
    hbm = pl.BlockSpec(memory_space=pl.ANY)
    vmem = pl.BlockSpec(memory_space=pltpu.VMEM)
    smem = pl.BlockSpec(memory_space=pltpu.SMEM)
    dma = pltpu.SemaphoreType.DMA

    def chunks(widths, *shape):
        return [pltpu.VMEM((*shape, width), BF) for width in widths]

    halves = [width // 2 for width in WIDTHS]
    carried = [*WIDTHS[:-1], WIDTHS[-1] + EXTRA]
    scratch = [
        pltpu.VMEM((512, 256), BF),
        pltpu.VMEM((32, 512), BF),
        pltpu.VMEM((32, 512), BF),
        pltpu.VMEM((256, D), BF),
        pltpu.VMEM((32, D), BF),
        pltpu.VMEM((1, 2 * FF, D), BF),
        pltpu.VMEM((1, FF, D), BF),
        pltpu.VMEM((D,), F32),
        pltpu.VMEM((4, 32), jnp.int32),
        pltpu.VMEM((4, 32), F32),
        pltpu.VMEM((2, 64, 640), BF),
        pltpu.VMEM((4, 128, 512), BF),
        pltpu.VMEM((4, 128, 512), BF),
        pltpu.VMEM((512, 256), BF),
        pltpu.VMEM((32, D), F32),
        pltpu.VMEM((8, 8, 256), F32),
        pltpu.VMEM((256, 256), BF),
        pltpu.VMEM((2, 256, 256), BF),
        pltpu.VMEM((256, FF), F32),
        pltpu.VMEM((256, FF), F32),
        pltpu.VMEM((256, FF), BF),
        *chunks(halves, 2, 4, 128),
        *chunks(halves, 4, 128),
        *chunks(halves, 4, 4, 32),
        *chunks(halves, 128),
        *chunks(halves, 4, 32),
        *chunks(halves, 4, 32),
        *chunks(halves, 4, 32),
        *chunks(carried, 256) * 3,
        *chunks(BACK, 256) * 2,
        *chunks(BACK, 4, 2, 32),
        *chunks(BACK, 4, 32) * 3,
        dma((10,)),
        dma((3,)),
        dma((3,)),
        *[dma((CHUNKS, 2))] * 4,
        dma((1,)),
        dma((1,)),
        dma((2, CHUNKS)),
        dma((2, CHUNKS)),
        dma((CHUNKS,)),
        dma((CHUNKS, 4)),
        *[dma((CHUNKS,))] * 6,
    ]
    return pl.pallas_call(
        layer_kernel,
        out_shape=jax.ShapeDtypeStruct((32, D), BF),
        in_specs=[hbm, hbm, hbm, smem, hbm, hbm, hbm, hbm, hbm, hbm, hbm],
        out_specs=vmem,
        scratch_shapes=scratch,
        compiler_params=pltpu.CompilerParams(
            collective_id=1, has_side_effects=True, vmem_limit_bytes=60 * 1024 * 1024
        ),
        name="layer",
    )(
        queries, key_rows.T, value_rows.T, sink_logits, out_proj, residual, norm_gain,
        expert_ids.T, gate_weights.T, jnp.swapaxes(w_gate_up, 1, 2), w_down,
    )


def solution(mesh):
    return jax.shard_map(
        per_device,
        mesh=mesh,
        in_specs=(
            P("seq", "exp"),
            P("seq", "exp"),
            P("seq", "exp"),
            P("exp"),
            P("exp", None),
            P(("seq", "exp"), None),
            P(),
            P(("seq", "exp"), None),
            P(("seq", "exp"), None),
            P(("seq", "exp"), None, None),
            P(("seq", "exp"), None, None),
        ),
        out_specs=P(("seq", "exp"), None),
        check_vma=False,
    )
```

time: 85.9 us -> 80.2 us (0.934)
  Pallas kernels: 84.1 us -> 78.4 us
    pallas_call x1, Pallas kernels: 84.1 us -> 78.4 us  [per_device(): pl.pallas_call(layer_kernel, out_shape=jax.ShapeDtypeStruct((32, D), BF),...]
where the time goes in v5:
time: 80.2 us; the launch traced here: 80 us
  Pallas kernels  78.4 us (98%)
  local copies, waits for them, and re-layouts  1.59 us (2%)
    pallas_call x1, Pallas kernels, per_device(): pl.pallas_call(layer_kernel, out_shape=jax.ShapeDtypeStruct((32, D), BF),...  78.4 us

profile of v5, /device:TPU:1, one launch (start us, length us, event | category | flops | bytes accessed | tf_op | source)
XLA Modules:
  0.0 80.0 jit_solution(17293437842948594863)
XLA Ops:
  0.0 78.4 %layer.1 = bf16[32,2560]{1,0:T(8,128)(2,1)} custom-call(bf16[512,256]{1,0:T(8,128)(2,1)} %q_hbm.1, bf16[32,512]{1,0:T(8,128)(2,1)} %bitcast.6, bf16[32,512]{1,0:T(8,128)(2,1)} %bitcast.7, f32[4]{0:T(128)} %sink_ref.1, bf16[256,2560]{1,0:T(8,128)(2,1)} %wo_hbm.1, bf16[32,2560]{1,0:T(8,128)(2,1)} %res_hbm.1, f32[2560]{0:T(1024)} %gain_hbm.1, s32[4,32]{1,0:T(4,128)} %bitcast.8, ...), custom_call_target="tpu_custom_call" | custom-call | tf_op jit(solution)/shard_map/layer/pallas_call | solution.py:492
  78.4 1.6 %copy.13 = bf16[32,2560]{1,0:T(8,128)(2,1)} copy(bf16[32,2560]{1,0:T(8,128)(2,1)} %layer.1) | data formatting | bytes 327680

commit v6 on v5

--- a/solution.py
+++ b/solution.py
@@ -14,9 +14,14 @@
 FF = 1440
 COL = 256
 EXTRA = 128
-WIDTHS = (512, 512, 768, 512, 256)
-BACK = (256, 768, 768, 512, 256)
+WIDTHS = (256, 512, 512, 512, 512, 256)
+BACK = (256, 512, 512, 512, 512, 256)
 CHUNKS = len(WIDTHS)
+ORDER = (
+    "P0", "P1", "P2", "P3", "M0", "M1", "M2", "M3", "S0", "P4", "S1", "P5", "S2", "S3", "T0",
+    "M4", "T1", "M5", "R0", "T2", "T3", "S4", "G0", "S5", "R1", "R2", "T4", "G1", "R3", "G2",
+    "T5", "G3", "R4", "R5", "G4", "G5",
+)
 
 
 def mm(a, b):
@@ -50,20 +55,21 @@
 
 
 def layer_kernel(
-    q_hbm, k_hbm, v_hbm, sink_ref, wo_hbm, res_hbm, gain_hbm, ids_hbm, gates_hbm, wgu_hbm, wd_hbm, out_ref, *scratch
+    q_hbm, k_hbm, v_hbm, sink_hbm, wo_hbm, res_hbm, gain_hbm, ids_hbm, gates_hbm, wgu_hbm, wd_hbm, out_ref, *scratch
 ):
     take = iter(scratch)
 
     def per_chunk():
         return [next(take) for _ in range(CHUNKS)]
 
-    q, kraw, vraw, wo, res, wgu, wd, gain_ref, ids_ref, gates_ref = [next(take) for _ in range(10)]
+    q, kraw, vraw, wo, res, wgu, wd, gain_ref, ids_ref, gates_ref, sinks = [next(take) for _ in range(11)]
     kext, bdk, bdv, att, hidden, metas, select, weigh, acc_gate, acc_lift, act = [next(take) for _ in range(11)]
-    shares, recv_z, recv_x, sum_a, sum_b, recv_a2, recv_b2 = [per_chunk() for _ in range(7)]
+    shares, via_a, via_b, recv_z, recv_x, sum_a, sum_b, recv_a2, recv_b2 = [per_chunk() for _ in range(9)]
+    via = (via_a, via_b)
     tokens, slots, rows_in = [per_chunk() for _ in range(3)]
     rows_out, answers, partial, crossed, summed, returned = [per_chunk() for _ in range(6)]
-    load_sem, kv_send, kv_recv, first_send, first_recv, second_send, second_recv = [next(take) for _ in range(7)]
-    meta_send, meta_recv, ex_send, ex_recv, gather_send, gather_recv = [next(take) for _ in range(6)]
+    load_sem, kv_send, kv_recv, via_send, via_recv, first_send, first_recv = [next(take) for _ in range(7)]
+    second_send, second_recv, meta_send, meta_recv, ex_send, ex_recv, gather_send, gather_recv = [next(take) for _ in range(8)]
     relay_send, relay_recv, cross_send, cross_recv, home_send, home_recv = [next(take) for _ in range(6)]
     s = lax.axis_index("seq")
     e = lax.axis_index("exp")
@@ -77,27 +83,27 @@
     s_next = lax.rem(s + 1, 8)
     s_last = lax.rem(s + 7, 8)
 
+    barrier = pltpu.get_barrier_semaphore()
+
+    def greet(device):
+        pl.semaphore_signal(barrier, inc=1, device_id=device, device_id_type=MESH)
+
+    loop(1, 16, lambda d: greet((s, lax.rem(e + d, 16))))
+    loop(1, 8, lambda d: greet((lax.rem(s + d, 8), e)))
+    greet((s_next, mate))
+    greet((s_last, mate))
+
     loads = [
         pltpu.make_async_copy(a, b, load_sem.at[i])
         for i, (a, b) in enumerate(
             [
                 (k_hbm, kraw), (v_hbm, vraw), (q_hbm, q), (wo_hbm, wo), (res_hbm, res), (wgu_hbm, wgu), (wd_hbm, wd),
-                (gain_hbm, gain_ref), (ids_hbm, ids_ref), (gates_hbm, gates_ref),
+                (gain_hbm, gain_ref), (ids_hbm, ids_ref), (gates_hbm, gates_ref), (sink_hbm, sinks),
             ]
         )
     ]
-    for i in (0, 1, 8, 9, 2, 3, 7, 4, 5, 6):
+    for i in (0, 1, 2, 10, 8, 9, 3, 7, 4, 5, 6):
         loads[i].start()
-
-    barrier = pltpu.get_barrier_semaphore()
-
-    def greet(device):
-        pl.semaphore_signal(barrier, inc=1, device_id=device, device_id_type=MESH)
-
-    loop(1, 16, lambda d: greet((s, lax.rem(e + d, 16))))
-    loop(1, 8, lambda d: greet((lax.rem(s + d, 8), e)))
-    greet((s_next, mate))
-    greet((s_last, mate))
 
     loads[0].wait()
     kext[parity, 0:32, 128:640] = kraw[...]
@@ -134,8 +140,8 @@
 
     bdk[...] = jnp.zeros((4, 128, 512), BF)
     bdv[...] = jnp.zeros((4, 128, 512), BF)
-    loads[2].wait()
-    loads[3].wait()
+    for i in (2, 3, 10):
+        loads[i].wait()
     for c in kv_copies:
         c.wait_recv()
 
@@ -156,7 +162,7 @@
             scores = mm(queries, bdk[b]) * (1.0 / math.sqrt(64))
             probs = []
             for half in range(2):
-                sink = sink_ref[pair * 2 + half]
+                sink = sinks[pair * 2 + half]
                 part = jnp.where(allowed, scores[:, half * 256 : half * 256 + 256], -1e30)
                 highest = jnp.maximum(jnp.max(part, axis=1, keepdims=True), sink)
                 raised = jnp.exp(part - highest)
@@ -178,28 +184,50 @@
         wide = WIDTHS[c] // 2
         return slice(sum(WIDTHS[:c]) + half * wide, sum(WIDTHS[:c]) + half * wide + wide)
 
+    def z_peer(i):
+        return lax.rem(z + 1 + i, 4)
+
+    def x_peer(i):
+        return lax.rem(x + 1 + i, 4)
+
+    def rows_of(peer):
+        return pl.ds(aligned(peer * 32, 32), 32)
+
+    def piece(c, half, i):
+        return shares[c].at[0, z_peer(i)] if half == 0 else shares[c].at[1, :, rows_of(x_peer(i))]
+
+    def part_of(half, ref, p):
+        return ref.at[pl.ds(p * 64, 64)] if half == 0 else ref.at[pl.ds(p * 2, 2)]
+
+    def neighbour(half, side):
+        i = 2 * side
+        return (s, z_peer(i) * 4 + x) if half == 0 else (s, z * 4 + x_peer(i))
+
+    def via_copy(c, half, p):
+        src = part_of(half, piece(c, half, 1), p)
+        return remote(src, via[half][c].at[p], via_send.at[c, half], via_recv.at[c, half], neighbour(half, p))
+
+    def near_copy(c, half, side, p):
+        src = part_of(half, piece(c, half, 2 * side), p)
+        dst = part_of(half, (recv_z, recv_x)[half][c].at[side], p)
+        return remote(src, dst, first_send.at[c, half], first_recv.at[c, half], neighbour(half, side))
+
     def project(c):
         for half in range(2):
             share = mm(att[...], wo[:, half_columns(c, half)])
             shares[c][half] = share.reshape(4, 128, WIDTHS[c] // 2).astype(BF)
-            for i in range(3):
-                first_copy(c, half, i).start()
-
-    def z_peer(i):
-        return lax.rem(z + 1 + i, 4)
-
-    def x_peer(i):
-        return lax.rem(x + 1 + i, 4)
-
-    def rows_of(peer):
-        return pl.ds(aligned(peer * 32, 32), 32)
-
-    def first_copy(c, half, i):
-        if half == 0:
-            src, dst, peer = shares[c].at[0, z_peer(i)], recv_z[c].at[z], z_peer(i) * 4 + x
-        else:
-            src, dst, peer = shares[c].at[1, :, rows_of(x_peer(i))], recv_x[c].at[x], z * 4 + x_peer(i)
-        return remote(src, dst, first_send.at[c, half], first_recv.at[c, half], (s, peer))
+            for p in range(2):
+                via_copy(c, half, p).start()
+            for p in range(2):
+                near_copy(c, half, 1 - p, p).start()
+
+    def merge(c):
+        for half in range(2):
+            arrived(via[half][c], via_recv.at[c, half])
+            for p in range(2):
+                own = part_of(half, piece(c, half, 2 * p), p)
+                own[...] = (own[...].astype(F32) + via[half][c][p].astype(F32)).astype(BF)
+                near_copy(c, half, p, p).start()
 
     def second_copy(c, half, i):
         if half == 0:
@@ -209,17 +237,17 @@
         return remote(src, dst, second_send.at[c, half], second_recv.at[c, half], (s, peer))
 
     def sum_first(c):
-        arrived(recv_z[c].at[pl.ds(0, 3)], first_recv.at[c, 0])
+        arrived(recv_z[c], first_recv.at[c, 0])
         total = shares[c][0, z].astype(F32)
-        for i in range(3):
-            total = total + recv_z[c][z_peer(i)].astype(F32)
+        for side in range(2):
+            total = total + recv_z[c][side].astype(F32)
         sum_a[c][...] = total.astype(BF)
         for i in range(3):
             second_copy(c, 0, i).start()
-        arrived(recv_x[c].at[pl.ds(0, 3)], first_recv.at[c, 1])
+        arrived(recv_x[c], first_recv.at[c, 1])
         total = shares[c][1, :, rows_of(x), :].astype(F32)
-        for i in range(3):
-            total = total + recv_x[c][x_peer(i)].astype(F32)
+        for side in range(2):
+            total = total + recv_x[c][side].astype(F32)
         sum_b[c][...] = total.astype(BF)
         for i in range(3):
             second_copy(c, 1, i).start()
@@ -328,8 +356,13 @@
             up_tile(c, n * COL, COL, scale)
         up_tile(c, 5 * COL, FF - 5 * COL, scale)
 
-    project(0)
-    project(1)
+    def run(names):
+        steps = {"P": project, "M": merge, "S": sum_first, "T": sum_second, "R": relay, "G": dispatch}
+        for name in names:
+            steps[name[0]](int(name[1]))
+
+    run(ORDER[:2])
+
     arrived(metas.at[pl.ds(0, 7)], meta_recv.at[0])
     meta = metas[0]
     for i in range(1, 8):
@@ -356,21 +389,7 @@
     loads[4].wait()
     loads[7].wait()
     gain = gain_ref[...].reshape(1, D)
-    for c in range(CHUNKS):
-        sum_first(c)
-        if c + 2 < CHUNKS:
-            project(c + 2)
-        if c >= 1:
-            sum_second(c - 1)
-        if c >= 2:
-            relay(c - 2)
-        if c >= 3:
-            dispatch(c - 3)
-    sum_second(4)
-    for c in range(3, CHUNKS):
-        relay(c)
-        dispatch(c - 1)
-    dispatch(4)
+    run(ORDER[2:])
     loads[5].wait()
     for c in range(CHUNKS):
         up(c)
@@ -408,8 +427,10 @@
         c.wait_send()
     arrived(metas.at[pl.ds(0, 7)], meta_send.at[0])
     for c in range(CHUNKS):
-        arrived(recv_z[c].at[pl.ds(0, 3)], first_send.at[c, 0])
-        arrived(recv_x[c].at[pl.ds(0, 3)], first_send.at[c, 1])
+        arrived(recv_z[c], first_send.at[c, 0])
+        arrived(recv_x[c], first_send.at[c, 1])
+        for half in range(2):
+            arrived(via[half][c], via_send.at[c, half])
         arrived(recv_a2[c].at[pl.ds(0, 3)], second_send.at[c, 0])
         arrived(recv_b2[c].at[pl.ds(0, 3)], second_send.at[c, 1])
         arrived(tokens[c].at[pl.ds(0, 128)], gather_send.at[c])
@@ -436,7 +457,6 @@
 ):
     hbm = pl.BlockSpec(memory_space=pl.ANY)
     vmem = pl.BlockSpec(memory_space=pltpu.VMEM)
-    smem = pl.BlockSpec(memory_space=pltpu.SMEM)
     dma = pltpu.SemaphoreType.DMA
 
     def chunks(widths, *shape):
@@ -455,6 +475,7 @@
         pltpu.VMEM((D,), F32),
         pltpu.VMEM((4, 32), jnp.int32),
         pltpu.VMEM((4, 32), F32),
+        pltpu.SMEM((4,), F32),
         pltpu.VMEM((2, 64, 640), BF),
         pltpu.VMEM((4, 128, 512), BF),
         pltpu.VMEM((4, 128, 512), BF),
@@ -467,8 +488,10 @@
         pltpu.VMEM((256, FF), F32),
         pltpu.VMEM((256, FF), BF),
         *chunks(halves, 2, 4, 128),
-        *chunks(halves, 4, 128),
-        *chunks(halves, 4, 4, 32),
+        *chunks(halves, 2, 64),
+        *chunks(halves, 2, 2, 32),
+        *chunks(halves, 2, 128),
+        *chunks(halves, 2, 4, 32),
         *chunks(halves, 128),
         *chunks(halves, 4, 32),
         *chunks(halves, 4, 32),
@@ -477,10 +500,10 @@
         *chunks(BACK, 256) * 2,
         *chunks(BACK, 4, 2, 32),
         *chunks(BACK, 4, 32) * 3,
-        dma((10,)),
+        dma((11,)),
         dma((3,)),
         dma((3,)),
-        *[dma((CHUNKS, 2))] * 4,
+        *[dma((CHUNKS, 2))] * 6,
         dma((1,)),
         dma((1,)),
         dma((2, CHUNKS)),
@@ -491,8 +514,8 @@
     ]
     return pl.pallas_call(
         layer_kernel,
-        out_shape=jax.ShapeDtypeStruct((32, D), BF),
-        in_specs=[hbm, hbm, hbm, smem, hbm, hbm, hbm, hbm, hbm, hbm, hbm],
+        out_shape=pltpu.VMEM((32, D), BF),
+        in_specs=[hbm, hbm, hbm, hbm, hbm, hbm, hbm, hbm, hbm, hbm, hbm],
         out_specs=vmem,
         scratch_shapes=scratch,
         compiler_params=pltpu.CompilerParams(

time: 80.2 us -> 76 us (0.948)
  Pallas kernels: 78.4 us -> 75.3 us
  local copies, waits for them, and re-layouts: 1.59 us -> 0.67 us
    pallas_call x1, Pallas kernels: 78.4 us -> 75.3 us  [per_device(): pl.pallas_call(layer_kernel, out_shape=pltpu.VMEM((32, D), BF), in_specs=...]
    unnamed x1, local copies, waits for them, and re-layouts: 1.59 us -> 0.67 us
where the time goes in v6:
time: 76 us; the launch traced here: 75.9 us
  Pallas kernels  75.3 us (99%)
    pallas_call x1, Pallas kernels, per_device(): pl.pallas_call(layer_kernel, out_shape=pltpu.VMEM((32, D), BF), in_specs=...  75.3 us

profile of v6, /device:TPU:1, one launch (start us, length us, event | category | flops | bytes accessed | tf_op | source)
XLA Modules:
  0.0 75.9 jit_solution(11030805571118604123)
XLA Ops:
  0.0 75.3 %layer.1 = bf16[32,2560]{1,0:T(8,128)(2,1)S(1)} custom-call(bf16[512,256]{1,0:T(8,128)(2,1)} %q_hbm.1, bf16[32,512]{1,0:T(8,128)(2,1)} %bitcast.6, bf16[32,512]{1,0:T(8,128)(2,1)} %bitcast.7, f32[4]{0:T(128)} %sink_hbm.1, bf16[256,2560]{1,0:T(8,128)(2,1)} %wo_hbm.1, bf16[32,2560]{1,0:T(8,128)(2,1)} %res_hbm.1, f32[2560]{0:T(1024)} %gain_hbm.1, ...), custom_call_target="tpu_custom_call" | custom-call | tf_op jit(solution)/shard_map/layer/pallas_call | solution.py:515
  75.3 0.7 copy.13
